TPU v7x, 256 devices: a whole 4x4x8 slice. The times are simulated.
256 devices in a mesh: rep: 8 (over z_lo, core), dp: 32 (over z_hi, x, y).
Axes of the slice: x: 4, y: 4, z: 8 (z_hi: 2, z_lo: 4; z = z_hi * 4 + z_lo), core: 2. Of those that a mesh axis runs over, the one named last changes fastest.
Arguments:
- hidden: bfloat16 [2, 8, 16384, 1920], P(None, 'rep', 'dp'), may hold values from -6 to 6
- partners: int32 [2, 8], replicated, may hold values from 0 to 7, as said below
- frame_mask: int32 [2, 16384], P(None, 'dp'), may hold values 0 or 1
- segment_ids: int32 [2, 16384], P(None, 'dp'), may hold values from 0 to 7, as said below
- master: float32 [8, 1920, 500], P('rep', 'dp'), may hold values from -0.125 to 0.125
- moment_one: float32 [8, 1920, 500], P('rep', 'dp'), may hold values from -3 to 3
- moment_two: float32 [8, 1920, 500], P('rep', 'dp'), may hold values from 0.1 to 10
Outputs:
- hidden_grad: bfloat16 [2, 8, 16384, 1920], P(None, 'rep', 'dp')
- new_master: float32 [8, 1920, 500], P('rep', 'dp')
- new_moment_one: float32 [8, 1920, 500], P('rep', 'dp')
- new_moment_two: float32 [8, 1920, 500], P('rep', 'dp')
Inputs may be any that keep to these rules, and one draw needn't show every extreme that they name: `partners`: each row is a permutation of the replicas forming one cycle through all of them, so no replica is its own partner. `segment_ids`: within each aligned block of 512 frames the ids start at 0 and never fall.
All inputs are finite; a program needn't handle non-finite values. No bound on the sum of `frame_mask` on one device may be relied on, other than what follows from the above.
Results may differ from a plain program's by a relative error of at most 0.035.
Values may be sent and summed in bfloat16 or wider, within the bound.
A program may use at most 64 MiB of HBM per device.

v0:
```python
import jax
import jax.numpy as jnp
from jax import lax
from jax.sharding import Mesh
from jax.sharding import PartitionSpec as P

SEGS = 8
DP = ("dp_0", "dp_1", "dp_2")


def joined_along(tiles, dim):
    tiles = jnp.moveaxis(tiles, 0, dim)
    dims = tiles.shape
    return tiles.reshape(*dims[:dim], dims[dim] * dims[dim + 1], *dims[dim + 2 :])


def gather_in_order(x, axes, turns):
    tiles = x
    for k in turns:
        tiles = lax.all_gather(tiles, axes[k])
    done = turns[::-1]
    back = [done.index(k) for k in range(len(axes))]
    tiles = tiles.transpose(*back, *range(len(axes), tiles.ndim))
    return tiles.reshape(-1, *x.shape)


def whole_of(x, axes, turns, dim):
    return joined_along(gather_in_order(x, axes, turns), dim)


def sum_in_order(tiles, axes, turns):
    inside = tiles.shape[1:]
    tiles = tiles.reshape(*(lax.axis_size(a) for a in axes), *inside)
    tiles = jnp.moveaxis(tiles, turns, range(len(axes))).reshape(-1, *inside)
    for k in turns:
        tiles = lax.psum_scatter(tiles, axes[k], scatter_dimension=0, tiled=True)
    return tiles[0]


def split_up(x, dim, devices):
    before, after = (x.shape[:dim], x.shape[dim + 1 :])
    return jnp.moveaxis(x.reshape(*before, devices, -1, *after), dim, 0)


def summed_rows(x, axes, turns, dim):
    devices = lax.axis_size(axes)
    return sum_in_order(split_up(x, dim, devices), axes, turns)


def per_device(hidden, partners, frame_mask, segment_ids, master, moment_one, moment_two):
    frame_count = hidden.shape[2]
    feature_dim = hidden.shape[3]
    head_low = master.astype(jnp.bfloat16)
    head_full = whole_of(head_low, DP, (0, 1, 2), 1)[0]
    frames_all = hidden[:, 0].reshape(2 * frame_count, feature_dim)
    logits = jnp.dot(frames_all, head_full, preferred_element_type=jnp.float32)
    logits = logits.reshape(2, frame_count, head_full.shape[1])
    sent = logits.astype(jnp.bfloat16)[None]
    mine = lax.axis_index("rep")
    partner_now = partners[:, mine]
    piece = lax.all_gather(sent, "rep", axis=0, tiled=True)
    offsets = jnp.arange(piece.shape[0], dtype=jnp.int32)
    selector = (offsets[:, None] == partner_now[None, :]).astype(jnp.bfloat16)
    other = jnp.einsum("km,kmtv->mtv", selector, piece, preferred_element_type=jnp.float32)
    valid = frame_mask.astype(jnp.float32)
    onehot = (segment_ids[..., None] == jnp.arange(SEGS, dtype=jnp.int32)).astype(jnp.float32)
    counts = jnp.sum(onehot * valid[..., None], axis=1)
    per_frame = jnp.sum(onehot * counts[:, None, :], axis=-1)
    scale = valid / jnp.maximum(per_frame, 1.0)
    grad = ((logits - other) * scale[:, :, None]).astype(jnp.bfloat16)
    grad_all = grad.reshape(2 * frame_count, grad.shape[2])
    hidden_grad = jnp.einsum("tv,dv->td", grad_all, head_full, preferred_element_type=jnp.float32)
    hidden_grad = hidden_grad.astype(jnp.bfloat16).reshape(2, 1, frame_count, feature_dim)
    head_grad = summed_rows(
        jnp.einsum("td,tv->dv", frames_all, grad_all, preferred_element_type=jnp.float32).astype(
            jnp.bfloat16
        ),
        DP,
        (1, 2, 0),
        0,
    ).astype(jnp.float32)
    head_grad = head_grad[None]
    new_moment_one = 0.9 * moment_one + 0.1 * head_grad
    new_moment_two = 0.99 * moment_two + 0.01 * head_grad * head_grad
    new_master = master - 0.01 * new_moment_one / (jnp.sqrt(new_moment_two) + 1e-08)
    return (hidden_grad, new_master, new_moment_one, new_moment_two)


def solution(mesh):
    torus = Mesh(mesh.devices.reshape(mesh.shape["rep"], 2, 4, 4), ("rep", "dp_0", "dp_1", "dp_2"))
    in_specs = (
        P(None, "rep", DP, None),
        P(),
        P(None, DP),
        P(None, DP),
        P("rep", DP, None),
        P("rep", DP, None),
        P("rep", DP, None),
    )
    out_specs = (
        P(None, "rep", DP, None),
        P("rep", DP, None),
        P("rep", DP, None),
        P("rep", DP, None),
    )
    return jax.shard_map(
        per_device, mesh=torus, in_specs=in_specs, out_specs=out_specs, check_vma=False
    )
```

profile of v0, /device:TPU:32, one launch (start us, length us, event | category | flops | bytes accessed | tf_op | source)
XLA Modules:
  0.0 338.2 jit_solution(11109412332080898184)
XLA Ops:
  7.2 0.0 copy-start
  7.2 0.0 all-gather.7.cloned.1.call-start
  7.2 0.9 copy.76
  8.1 10.2 %all-gather = bf16[2,60,500]{2,1,0:T(8,128)(2,1)S(1)} all-gather(bf16[1,60,500]{2,1,0:T(8,128)(2,1)S(1)} %copy.76), channel_id=2, replica_groups=mesh['rep'=8,'dp_0'=2,'dp_1'=4,'dp_2'=4] {'dp_0'}, dimensions={0}, use_global_device_ids=true | all-gather | bytes 180000 | tf_op jit(solution)/shard_map/all_gather | solution.py:20
  18.3 13.7 %all-gather.1 = bf16[8,60,500]{2,1,0:T(8,128)(2,1)S(1)} all-gather(bf16[2,60,500]{2,1,0:T(8,128)(2,1)S(1)} %all-gather), channel_id=3, replica_groups=mesh['rep'=8,'dp_0'=2,'dp_1'=4,'dp_2'=4] {'dp_1'}, dimensions={0}, use_global_device_ids=true | all-gather | bytes 600000 | tf_op jit(solution)/shard_map/all_gather | solution.py:20
  32.0 1.3 copy.42
  33.3 0.0 all-gather.7.cloned.1.call-update
  33.3 0.0 all-gather.9.cloned.1.call-start
  33.4 33.5 %all-gather.7.cloned.1.call-done = bf16[16,2,1,60,500]{4,1,3,2,0:T(2,128)(2,1)} async-done(((bf16[4,2,1,60,500]{4,1,3,2,0:T(2,128)(2,1)}), bf16[16,2,1,60,500]{4,1,3,2,0:T(2,128)(2,1)}) %all-gather.7.cloned.1.call-update) | async-done | bytes 1920016 | tf_op jit(solution)/shard_map/all_gather | solution.py:20
  66.9 2.0 copy.43
  68.8 1.9 squeeze_reshape_transpose_reshape.3
  70.7 6.1 %fusion.17 = (bf16[2,512,500]{1,2,0:T(8,128)(2,1)}, f32[2,512,500]{1,2,0:T(8,128)S(1)}) fusion(bf16[1920,500]{1,0:T(8,128)(2,1)} %squeeze_reshape_transpose_reshape.3, bf16[2,1,512,1920]{3,2,1,0:T(8,128)(2,1)} %param.7), kind=kOutput, calls=%fused_computation.32 | convolution fusion | flops 1966592000 | bytes 8924160 | tf_op jit(solution)/shard_map/dot_general | solution.py:56
  76.8 0.0 all-gather.9.cloned.1.call-update
  76.9 0.2 all-reduce.5.cloned.1.call-start
  77.1 0.0 copy-done.6
  77.1 0.2 dynamic-slice_reduce_fusion
  77.3 0.1 fusion.18
  77.5 88.5 %all-gather.9.cloned.1.call-done = bf16[16,512,500]{1,2,0:T(8,128)(2,1)} async-done(((bf16[2,512,500]{1,2,0:T(8,128)(2,1)}), bf16[16,512,500]{1,2,0:T(8,128)(2,1)}) %all-gather.9.cloned.1.call-update) | async-done | bytes 8192016 | tf_op jit(solution)/shard_map/all_gather | solution.py:61
  165.9 5.3 %multiply_reduce_fusion = f32[2,512,500]{1,2,0:T(8,128)S(1)} fusion(bf16[2,8,512,500]{2,3,0,1:T(8,128)(2,1)} %bitcast.42, f32[2,8]{0,1:T(8,128)S(1)} %fusion.13), kind=kLoop, calls=%fused_computation.1 | loop fusion | flops 11776000 | bytes 10240064 | tf_op jit(solution)/shard_map/km,kmtv->mtv/dot_general | solution.py:64
  171.3 0.6 multiply_convert_fusion
  171.9 1.3 copy.45
  173.2 4.8 %fusion.3 = bf16[1920,500]{0,1:T(8,128)(2,1)S(1)} fusion(bf16[1024,500]{1,0:T(8,128)(2,1)} %bitcast.45, bf16[1024,1920]{1,0:T(8,128)(2,1)} %bitcast.47), kind=kOutput, calls=%fused_computation.6 | convolution fusion | flops 1967040000 | bytes 6876160 | tf_op jit(solution)/shard_map/td,tv->dv/dot_general | solution.py:75
  178.0 2.3 copy.47
  180.3 2.8 reshape_reshape.3
  183.2 3.3 copy.48
  186.5 5.3 %reshape.30 = bf16[32,60,500]{2,0,1:T(8,128)(2,1)} reshape(bf16[4,4,2,60,500]{4,2,1,0,3:T(2,128)(2,1)} %copy.48) | data formatting | bytes 3840000 | tf_op jit(solution)/shard_map/reshape | solution.py:34
  191.9 0.0 all-reduce.5.cloned.1.call-update
  191.9 0.0 all-reduce.7.cloned.1.call-start
  192.0 0.6 dynamic-slice
  193.4 62.7 %all-reduce.5.cloned.1.call-done = bf16[32,60,500]{2,0,1:T(8,128)(2,1)} async-done(((bf16[32,60,500]{2,0,1:T(8,128)(2,1)}), bf16[32,60,500]{2,0,1:T(8,128)(2,1)}) %all-reduce.5.cloned.1.call-update) | async-done | bytes 1920016
  256.2 1.8 constant_dynamic-slice_fusion.1
  258.0 0.0 all-reduce.7.cloned.1.call-update
  258.0 0.3 reduce-scatter.4.cloned.1.call-start
  258.3 0.6 dynamic-slice.2
  259.5 46.6 %all-reduce.7.cloned.1.call-done = bf16[8,60,500]{2,0,1:T(8,128)(2,1)} async-done(((bf16[8,60,500]{2,0,1:T(8,128)(2,1)}), bf16[8,60,500]{2,0,1:T(8,128)(2,1)}) %all-reduce.7.cloned.1.call-update) | async-done | bytes 480016
  306.2 1.2 constant_dynamic-slice_fusion
  307.3 0.7 copy.49
  308.0 0.0 reduce-scatter.4.cloned.1.call-update
  308.0 0.0 copy-done.1
  308.0 0.0 copy-start.3
  308.1 0.0 copy-start.4
  308.1 0.0 copy-start.5
  308.1 4.3 %convolution_convert_fusion = bf16[1024,1920]{1,0:T(8,128)(2,1)} fusion(bf16[1024,500]{1,0:T(8,128)(2,1)S(1)} %bitcast.46, bf16[1920,500]{1,0:T(8,128)(2,1)S(1)} %copy-done.1), kind=kOutput, calls=%fused_computation.4 | convolution fusion | flops 1968046080 | bytes 6876160 | tf_op jit(solution)/shard_map/tv,dv->td/dot_general | solution.py:72
  312.4 16.0 %reduce-scatter.4.cloned.1.call-done = bf16[1,60,500]{2,1,0:T(8,128)(2,1)} async-done(((bf16[2,60,500]{2,1,0:T(8,128)(2,1)}), bf16[1,60,500]{2,1,0:T(8,128)(2,1)}) %reduce-scatter.4.cloned.1.call-update) | async-done | bytes 60016 | tf_op jit(solution)/shard_map/reduce_scatter | solution.py:36
  328.4 0.9 divide_subtract_fusion
  329.3 0.8 copy.53
  330.1 0.8 copy.54
  330.9 0.8 copy.55
  (17 shorter events, 0.0 us)
Async XLA Ops:
  7.2 70.0 %copy-start = (s32[2,8]{1,0:T(2,128)S(1)}, s32[2,8]{1,0:T(2,128)}, u32[]{:S(2)}) copy-start(s32[2,8]{1,0:T(2,128)} %param.8) | copy-start | bytes 196
  7.2 59.7 %all-gather.7.cloned.1.call-start = ((), (), s32[]{:S(2)}) async-start(), calls=%async_computation.2 | async-start | bytes 2457600 | tf_op jit(solution)/shard_map/all_gather | solution.py:20
  33.3 132.6 %all-gather.9.cloned.1.call-start = ((), (), s32[]{:S(2)}) async-start(), calls=%async_computation.3 | async-start | bytes 9289728 | tf_op jit(solution)/shard_map/all_gather | solution.py:61
  70.7 6.4 %copy-start.6 = (s32[2,512]{1,0:T(2,128)S(1)}, s32[2,512]{1,0:T(2,128)}, u32[]{:S(2)}) copy-start(s32[2,512]{1,0:T(2,128)} %param.9) | copy-start | bytes 12292
  70.7 6.6 %copy-start.7 = (s32[2,512]{1,0:T(2,128)S(1)}, s32[2,512]{1,0:T(2,128)}, u32[]{:S(2)}) copy-start(s32[2,512]{1,0:T(2,128)} %param.10) | copy-start | bytes 12292
  76.9 179.3 %all-reduce.5.cloned.1.call-start = ((), (), s32[]{:S(2)}) async-start(), calls=%async_computation.4 | async-start | bytes 3932160
  186.5 5.4 %copy-start.9 = (u32[256]{0:T(256)S(1)}, u32[256]{0:T(256)}, u32[]{:S(2)}) copy-start(u32[256]{0:T(256)} %constant.33) | copy-start | bytes 3076
  191.9 66.4 %copy-start.8 = (u32[256]{0:T(256)S(1)}, u32[256]{0:T(256)}, u32[]{:S(2)}) copy-start(u32[256]{0:T(256)} %constant.37) | copy-start | bytes 3076
  191.9 116.2 %copy-start.1 = (bf16[1920,500]{1,0:T(8,128)(2,1)S(1)}, bf16[1920,500]{1,0:T(8,128)(2,1)}, u32[]{:S(2)}) copy-start(bf16[1920,500]{1,0:T(8,128)(2,1)} %squeeze_reshape_transpose_reshape.3) | copy-start | bytes 5760004
  191.9 116.2 %copy-start.2 = (bf16[2,512,500]{2,1,0:T(8,128)(2,1)S(1)}, bf16[2,512,500]{2,1,0:T(8,128)(2,1)}, u32[]{:S(2)}) copy-start(bf16[2,512,500]{2,1,0:T(8,128)(2,1)} %copy.45) | copy-start | bytes 3072004
  191.9 114.3 %all-reduce.7.cloned.1.call-start = ((), (), s32[]{:S(2)}) async-start(), calls=%async_computation.5 | async-start | bytes 983040
  258.0 70.4 %reduce-scatter.4.cloned.1.call-start = ((), (), s32[]{:S(2)}) async-start(), calls=%async_computation.1 | async-start | bytes 196608 | tf_op jit(solution)/shard_map/reduce_scatter | solution.py:36
  308.0 20.3 %copy-start.3 = (f32[1,60,500]{2,0,1:T(1,128)S(1)}, f32[1,60,500]{2,0,1:T(1,128)}, u32[]{:S(2)}) copy-start(f32[1,60,500]{2,0,1:T(1,128)} %param.11) | copy-start | bytes 360004
  308.1 20.3 %copy-start.4 = (f32[1,60,500]{2,0,1:T(1,128)S(1)}, f32[1,60,500]{2,0,1:T(1,128)}, u32[]{:S(2)}) copy-start(f32[1,60,500]{2,0,1:T(1,128)} %param.12) | copy-start | bytes 360004
  308.1 20.3 %copy-start.5 = (f32[1,60,500]{2,0,1:T(1,128)S(1)}, f32[1,60,500]{2,0,1:T(1,128)}, u32[]{:S(2)}) copy-start(f32[1,60,500]{2,0,1:T(1,128)} %param.13) | copy-start | bytes 360004
Sparse Core Ops, SparseCore 0:
  33.4 33.3 all-gather.6
  77.0 88.9 all-gather.8
  192.0 64.1 all-reduce.4
  258.4 47.7 all-reduce.6
  308.6 19.7 reduce-scatter.3
where the time goes:
time: 342 us; the launch traced here: 338 us
  waiting for transfers between devices  247 us (72%)
  local copies, waits for them, and re-layouts  28.6 us (8%)
  blocking collectives  23.9 us (7%)
  between operations  15.5 us (5%)
  matrix products  15.2 us (4%)
  other arithmetic  6.99 us (2%)
    unnamed x7, waiting for transfers between devices  109 us
    all_gather x1, waiting for transfers between devices, per_device(): piece = lax.all_gather(sent, 'rep', axis=0, tiled=True)  88.5 us
    all_gather x1, waiting for transfers between devices, gather_in_order(): tiles = lax.all_gather(tiles, axes[k])  33.5 us
    all_gather x2, blocking collectives, gather_in_order(): tiles = lax.all_gather(tiles, axes[k])  23.9 us
    reduce_scatter x1, waiting for transfers between devices, sum_in_order(): tiles = lax.psum_scatter(tiles, axes[k], scatter_dimension=0, tiled=True)  16 us
    unnamed x28, local copies, waits for them, and re-layouts  7.46 us
  transfers between devices with their start and end apart: 5, of which 5 were waited for; matrix products, arithmetic and copies ran while one was open for 2% of the time, Pallas kernels for 0%

commit v1 on v0

v1 whole, which is shorter than its diff:
```python
import functools

import jax
import jax.numpy as jnp
from jax import lax
from jax.experimental import pallas as pl
from jax.experimental.pallas import tpu as pltpu
from jax.sharding import Mesh
from jax.sharding import PartitionSpec as P

MESH = pl.DeviceIdType.MESH
F32 = jnp.float32
BF16 = jnp.bfloat16
SEGS = 8
REPS = 8
LANES = 128
CHUNK = 256
ROWS = 60
PAD = 64
GROUP = 4 * ROWS


def spread(transposed):
    shape = (4 * PAD, GROUP) if transposed else (GROUP, 4 * PAD)
    packed = lax.broadcasted_iota(jnp.int32, shape, 1 if transposed else 0)
    padded = lax.broadcasted_iota(jnp.int32, shape, 0 if transposed else 1)
    moved = packed
    for k in (1, 2, 3):
        moved = moved + jnp.where(packed >= k * ROWS, PAD - ROWS, 0)
    return jnp.where(moved == padded, 1.0, 0.0).astype(BF16)


def kernel(
    partners, mask, segs, master, mom1, mom2, hidden_hbm,
    hg_hbm, new_master, new_m1, new_m2,
    hid, hid_t, hp, head, logits, sent, got_0, got_1, got_2, got_3, stage, other, scale, grad, hg,
    dw, r1, s2, r2, s3, r3,
    local_sem, out_sem, z_s, z_r, a_s, a_r, b_s, b_r, p1_s, p1_r, p2_s, p2_r,
    c_s, c_r, d_s, d_r, e_s, e_r,
):
    zl, co = lax.axis_index("zl"), lax.axis_index("co")
    zh, x, y = lax.axis_index("zh"), lax.axis_index("x"), lax.axis_index("y")
    me = zl * 2 + co
    tokens = hid.shape[0] // 2
    part = tokens // REPS
    got = (got_0, got_1, got_2, got_3)

    load = pltpu.make_async_copy(hidden_hbm, hid, local_sem)
    load.start()

    def rep_of(d):
        to = lax.rem(me + d, REPS)
        return to, {"zl": to // 2, "co": lax.rem(to, 2)}

    def on(axis, d):
        if axis == "zh":
            to = 1 - zh
        else:
            to = lax.rem((x if axis == "x" else y) + d, 4)
        return to, {axis: to}

    barrier = pltpu.get_barrier_semaphore()
    peers = [on("zh", 1)[1]] + [on(a, d)[1] for a in ("x", "y") for d in (1, 2, 3)]
    peers += [rep_of(d)[1] for d in range(1, REPS)]
    for peer in peers:
        pl.semaphore_signal(barrier, inc=1, device_id=peer, device_id_type=MESH)

    low = master[...].astype(BF16)
    vocab = low.shape[1]
    for s in range(4):
        cols = min(LANES, vocab - s * LANES)
        piece = low[:, s * LANES : s * LANES + cols]
        if cols < LANES:
            piece = jnp.concatenate([piece, jnp.zeros((ROWS, LANES - cols), BF16)], axis=1)
        piece = jnp.concatenate([piece, jnp.zeros((PAD - ROWS, LANES), BF16)], axis=0)
        hp[s, zh, x, y] = piece

    pl.semaphore_wait(barrier, len(peers))

    def send(src, dst, send_sem, recv_sem, peer):
        copy = pltpu.make_async_remote_copy(
            src_ref=src, dst_ref=dst, send_sem=send_sem, recv_sem=recv_sem,
            device_id=peer, device_id_type=MESH,
        )
        copy.start()
        return copy

    started = []

    z_copies, a_copies, b_copies = {}, {}, {}
    for s in range(4):
        ref = hp.at[s, zh, x, y]
        z_copies[s] = send(ref, ref, z_s.at[s], z_r.at[s], on("zh", 1)[1])
    for s in range(4):
        z_copies[s].wait_recv()
        ref = hp.at[s, :, x, y]
        first = "x" if s % 2 == 0 else "y"
        a_copies[s] = [
            send(ref, ref, a_s.at[s, d - 1], a_r.at[s, d - 1], on(first, d)[1]) for d in (1, 2, 3)
        ]
    for s in range(4):
        for copy in a_copies[s]:
            copy.wait_recv()
        if s % 2 == 0:
            ref, second = hp.at[s, :, :, y], "y"
        else:
            ref, second = hp.at[s, :, x], "x"
        b_copies[s] = [
            send(ref, ref, b_s.at[s, d - 1], b_r.at[s, d - 1], on(second, d)[1]) for d in (1, 2, 3)
        ]

    for m in range(2):
        valid = mask[m : m + 1, :].astype(F32)
        ids = segs[m : m + 1, :]
        onehot = (lax.broadcasted_iota(jnp.int32, (SEGS, tokens), 0) == ids).astype(F32)
        counts = jnp.sum(onehot * valid, axis=1, keepdims=True)
        per_frame = jnp.sum(onehot * counts, axis=0, keepdims=True)
        row = valid / jnp.maximum(per_frame, 1.0)
        wide = jnp.broadcast_to(row, (LANES, tokens))
        scale[m * tokens : (m + 1) * tokens, :] = wide.T

    load.wait()

    @pl.loop(0, hid.shape[1] // LANES)
    def _(j):
        at = pl.ds(pl.multiple_of(j * LANES, LANES), LANES)
        hid_t[at, :] = hid[:, at].T

    pack = spread(False)
    p1, p2 = {}, {}
    for c in range(2):
        lanes = slice(c * CHUNK, (c + 1) * CHUNK)
        for s in (2 * c, 2 * c + 1):
            for copy in b_copies[s]:
                copy.wait_recv()

        @pl.loop(0, 8)
        def _(g):
            rows = pl.ds(pl.multiple_of(g * GROUP, 16), GROUP)
            for s in (2 * c, 2 * c + 1):
                block = hp[s, g // 4, lax.rem(g, 4)].reshape(4 * PAD, LANES)
                head[rows, s * LANES : (s + 1) * LANES] = jnp.dot(
                    pack, block, preferred_element_type=F32
                ).astype(BF16)

        for m in range(2):

            @pl.loop(0, 2)
            def _(t):
                rows = pl.ds(pl.multiple_of(m * tokens + t * 4 * part, 4 * part), 4 * part)
                block = jnp.dot(hid[rows, :], head[:, lanes], preferred_element_type=F32)
                block = block.reshape(4, part, CHUNK)
                logits[m, pl.ds(t * 4, 4), :, lanes] = block
                sent[m, pl.ds(t * 4, 4), :, lanes] = block.astype(BF16)

            u = 2 * c + m
            p1[u] = []
            for d in range(1, REPS):
                to, peer = rep_of(d)
                p1[u].append(
                    send(sent.at[m, to, :, lanes], got[u].at[me], p1_s.at[u, d - 1], p1_r.at[u, d - 1], peer)
                )
            got[u][me] = sent[m, me, :, lanes]

    for u in range(4):
        c, m = u // 2, u % 2
        lanes = slice(c * CHUNK, (c + 1) * CHUNK)
        for copy in p1[u]:
            copy.wait_recv()
        p2[u] = []
        for d in range(1, REPS):
            to, peer = rep_of(d)
            stage[u, d - 1] = got[u][partners[m, to]]
            p2[u].append(
                send(stage.at[u, d - 1], other.at[m, me, :, lanes], p2_s.at[u, d - 1], p2_r.at[u, d - 1], peer)
            )
        other[m, me, :, lanes] = got[u][partners[m, me]]

    grow = spread(True)

    def gradient(c):
        lanes = slice(c * CHUNK, (c + 1) * CHUNK)
        for m in range(2):
            for copy in p2[2 * c + m]:
                copy.wait_recv()

            @pl.loop(0, REPS)
            def _(k):
                rows = pl.ds(pl.multiple_of((m * REPS + k) * part, part), part)
                by = scale[rows, :]
                for s in (2 * c, 2 * c + 1):
                    at = slice(s * LANES, (s + 1) * LANES)
                    diff = logits[m, k, :, at] - other[m, k, :, at].astype(F32)
                    grad[rows, at] = (diff * by).astype(BF16)

        @pl.loop(0, 8)
        def _(g):
            rows = pl.ds(pl.multiple_of(g * GROUP, 16), GROUP)
            block = jnp.dot(hid_t[rows, :], grad[:, lanes], preferred_element_type=F32).astype(BF16)
            block = jnp.dot(grow, block, preferred_element_type=F32).astype(BF16)
            for s in range(2):
                dw[2 * c + s, g // 4, lax.rem(g, 4)] = block[:, s * LANES : (s + 1) * LANES].reshape(4, PAD, LANES)

        copies = {}
        for s in (2 * c, 2 * c + 1):
            copies[s] = []
            for d in (1, 2, 3):
                to, peer = on("y" if s % 2 == 0 else "x", d)
                src = dw.at[s, :, :, to] if s % 2 == 0 else dw.at[s, :, to]
                copies[s].append(send(src, r1.at[s, d - 1], c_s.at[s, d - 1], c_r.at[s, d - 1], peer))
        return copies

    def second(c, copies):
        after = {}
        for s in (2 * c, 2 * c + 1):
            for copy in copies[s]:
                copy.wait_recv()

            @pl.loop(0, 8)
            def _(g):
                i, k = g // 4, lax.rem(g, 4)
                own = dw[s, i, k, y] if s % 2 == 0 else dw[s, i, x, k]
                total = own.astype(F32)
                for d in range(3):
                    total = total + r1[s, d, i, k].astype(F32)
                s2[s, i, k] = total.astype(BF16)

            after[s] = []
            for d in (1, 2, 3):
                to, peer = on("x" if s % 2 == 0 else "y", d)
                after[s].append(
                    send(s2.at[s, :, to], r2.at[s, d - 1], d_s.at[s, d - 1], d_r.at[s, d - 1], peer)
                )
        return after

    def third(c, copies):
        last = {}
        for s in (2 * c, 2 * c + 1):
            for copy in copies[s]:
                copy.wait_recv()
            mine = x if s % 2 == 0 else y
            for i in range(2):
                total = s2[s, i, mine].astype(F32)
                for d in range(3):
                    total = total + r2[s, d, i].astype(F32)
                s3[s, i] = total.astype(BF16)
            last[s] = send(s3.at[s, 1 - zh], r3.at[s], e_s.at[s], e_r.at[s], on("zh", 1)[1])
        return last

    def adam(c, copies):
        for s in (2 * c, 2 * c + 1):
            copies[s].wait_recv()
            cols = min(LANES, vocab - s * LANES)
            at = slice(s * LANES, s * LANES + cols)
            total = s3[s, zh].astype(F32) + r3[s].astype(F32)
            g = total[:ROWS, :cols]
            one = 0.9 * mom1[:, at] + 0.1 * g
            two = 0.99 * mom2[:, at] + 0.01 * g * g
            new_m1[:, at] = one
            new_m2[:, at] = two
            new_master[:, at] = master[:, at] - 0.01 * one / (jnp.sqrt(two) + 1e-08)

    first_0 = gradient(0)
    second_0 = second(0, first_0)
    first_1 = gradient(1)
    third_0 = third(0, second_0)

    outs = []
    width = hid.shape[1] // 5
    height = hid.shape[0] // 4
    for t in range(4):
        rows = slice(t * height, (t + 1) * height)

        @pl.loop(0, 5)
        def _(n):
            at = pl.ds(pl.multiple_of(n * width, LANES), width)
            block = lax.dot_general(
                grad[rows, :], head[at, :], (((1,), (1,)), ((), ())), preferred_element_type=F32
            )
            hg[rows, at] = block.astype(BF16)

        out = pltpu.make_async_copy(hg.at[rows], hg_hbm.at[rows], out_sem.at[t])
        out.start()
        outs.append(out)
        if t == 1:
            second_1 = second(1, first_1)

    third_1 = third(1, second_1)
    adam(0, third_0)
    adam(1, third_1)

    for out in outs:
        out.wait()
    for group in (z_copies, third_0, third_1):
        started += list(group.values())
    for group in (a_copies, b_copies, p1, p2, first_0, first_1, second_0, second_1):
        for copies in group.values():
            started += copies
    for copy in started:
        copy.wait_send()


def per_device(hidden, partners, frame_mask, segment_ids, master, moment_one, moment_two):
    tokens, depth = hidden.shape[2:]
    frames = 2 * tokens
    part = tokens // REPS
    width = 4 * LANES
    vocab = master.shape[2]
    vmem = pl.BlockSpec(memory_space=pltpu.VMEM)
    hbm = pl.BlockSpec(memory_space=pl.ANY)
    small = jax.ShapeDtypeStruct((ROWS, vocab), F32)
    dma = pltpu.SemaphoreType.DMA
    hg, new_master, m1, m2 = pl.pallas_call(
        kernel,
        out_shape=(jax.ShapeDtypeStruct((frames, depth), BF16), small, small, small),
        in_specs=[pl.BlockSpec(memory_space=pltpu.SMEM)] + [vmem] * 5 + [hbm],
        out_specs=(hbm, vmem, vmem, vmem),
        scratch_shapes=[
            pltpu.VMEM((frames, depth), BF16),
            pltpu.VMEM((depth, frames), BF16),
            pltpu.VMEM((4, 2, 4, 4, PAD, LANES), BF16),
            pltpu.VMEM((depth, width), BF16),
            pltpu.VMEM((2, REPS, part, width), F32),
            pltpu.VMEM((2, REPS, part, width), BF16),
            pltpu.VMEM((REPS, part, CHUNK), BF16),
            pltpu.VMEM((REPS, part, CHUNK), BF16),
            pltpu.VMEM((REPS, part, CHUNK), BF16),
            pltpu.VMEM((REPS, part, CHUNK), BF16),
            pltpu.VMEM((4, REPS - 1, part, CHUNK), BF16),
            pltpu.VMEM((2, REPS, part, width), BF16),
            pltpu.VMEM((frames, LANES), F32),
            pltpu.VMEM((frames, width), BF16),
            pltpu.VMEM((frames, depth), BF16),
            pltpu.VMEM((4, 2, 4, 4, PAD, LANES), BF16),
            pltpu.VMEM((4, 3, 2, 4, PAD, LANES), BF16),
            pltpu.VMEM((4, 2, 4, PAD, LANES), BF16),
            pltpu.VMEM((4, 3, 2, PAD, LANES), BF16),
            pltpu.VMEM((4, 2, PAD, LANES), BF16),
            pltpu.VMEM((4, PAD, LANES), BF16),
            dma, dma((4,)),
            dma((4,)), dma((4,)),
            dma((4, 3)), dma((4, 3)),
            dma((4, 3)), dma((4, 3)),
            dma((4, 7)), dma((4, 7)),
            dma((4, 7)), dma((4, 7)),
            dma((4, 3)), dma((4, 3)),
            dma((4, 3)), dma((4, 3)),
            dma((4,)), dma((4,)),
        ],
        compiler_params=pltpu.CompilerParams(
            collective_id=0, has_side_effects=True, vmem_limit_bytes=56 << 20
        ),
        name="codistill",
    )(
        partners, frame_mask, segment_ids, master[0], moment_one[0], moment_two[0],
        hidden.reshape(frames, depth),
    )
    return hg.reshape(hidden.shape), new_master[None], m1[None], m2[None]


def solution(mesh):
    axes = ("zl", "co", "zh", "x", "y")
    torus = Mesh(mesh.devices.reshape(4, 2, 2, 4, 4), axes)
    rep, dp = ("zl", "co"), ("zh", "x", "y")
    in_specs = (
        P(None, rep, dp, None),
        P(),
        P(None, dp),
        P(None, dp),
        P(rep, dp, None),
        P(rep, dp, None),
        P(rep, dp, None),
    )
    out_specs = (
        P(None, rep, dp, None),
        P(rep, dp, None),
        P(rep, dp, None),
        P(rep, dp, None),
    )
    return jax.shard_map(
        per_device, mesh=torus, in_specs=in_specs, out_specs=out_specs, check_vma=False
    )
```

time: 342 us -> 121 us (0.35)
  waiting for transfers between devices: 247 us -> 0 us
  Pallas kernels: 0 us -> 107 us
  blocking collectives: 23.9 us -> 0 us
  local copies, waits for them, and re-layouts: 28.6 us -> 12.6 us
  matrix products: 15.2 us -> 0 us
  between operations: 15.5 us -> 0.64 us
  other arithmetic: 6.99 us -> 0 us
    all_gather x2 -> x0, waiting for transfers between devices: 122 us -> none  [the longest x1 88.5 us: per_device(): piece = lax.all_gather(sent, 'rep', axis=0, tiled=True)]
    unnamed x7 -> x0, waiting for transfers between devices: 109 us -> none
    pallas_call x0 -> x1, Pallas kernels: none -> 107 us  [per_device(): pl.pallas_call(kernel, out_shape=(jax.ShapeDtypeStruct((frames, depth), B...]
    all_gather x2 -> x0, blocking collectives: 23.9 us -> none  [gather_in_order(): tiles = lax.all_gather(tiles, axes[k])]
    reduce_scatter x1 -> x0, waiting for transfers between devices: 16 us -> none  [sum_in_order(): tiles = lax.psum_scatter(tiles, axes[k], scatter_dimension=0, tiled=True)]
    dot_general x3 -> x0, matrix products: 15.2 us -> none  [the longest x1 6.14 us: per_device(): logits = jnp.dot(frames_all, head_full, preferred_element_type=jnp.float32)]
    dot_general x1 -> x0, other arithmetic: 5.34 us -> none  [per_device(): jnp.einsum('km,kmtv->mtv', selector, piece, preferred_element_type=jnp.fl...]
    reshape x1 -> x0, local copies, waits for them, and re-layouts: 5.33 us -> none  [sum_in_order(): tiles = jnp.moveaxis(tiles, turns, range(len(axes))).reshape(-1, *inside)]
  transfers between devices with their start and end apart: 5 -> 0, of which waited for: 5 -> 0; matrix products, arithmetic and copies ran while one was open for 2% -> 0% of each run, Pallas kernels for 0% -> 0%
where the time goes in v1:
time: 121 us; the launch traced here: 120 us
  Pallas kernels  107 us (88%)
  local copies, waits for them, and re-layouts  12.6 us (10%)
    pallas_call x1, Pallas kernels, per_device(): pl.pallas_call(kernel, out_shape=(jax.ShapeDtypeStruct((frames, depth), B...  107 us
    unnamed x6, local copies, waits for them, and re-layouts  12.6 us

profile of v1, /device:TPU:32, one launch (start us, length us, event | category | flops | bytes accessed | tf_op | source)
XLA Modules:
  0.0 120.3 jit_solution(18338761134909100214)
XLA Ops:
  0.6 1.6 %copy.21 = f32[1,60,500]{2,1,0:T(8,128)} copy(f32[1,60,500]{2,0,1:T(1,128)} %param.11) | data formatting | bytes 240000
  2.2 1.7 %copy_bitcast_fusion = (f32[60,500]{1,0:T(8,128)}, f32[60,500]{1,0:T(8,128)}) fusion(f32[1,60,500]{2,0,1:T(1,128)} %param.13, f32[1,60,500]{2,0,1:T(1,128)} %param.12), kind=kLoop, calls=%fused_computation | loop fusion | bytes 480000
  3.9 107.1 %codistill.1 = (bf16[1024,1920]{1,0:T(8,128)(2,1)}, f32[60,500]{1,0:T(8,128)}, f32[60,500]{1,0:T(8,128)}, f32[60,500]{1,0:T(8,128)}) custom-call(s32[2,8]{1,0:T(2,128)} %partners.1, s32[2,512]{1,0:T(2,128)} %mask.1, s32[2,512]{1,0:T(2,128)} %segs.1, f32[60,500]{1,0:T(8,128)} %bitcast.16, f32[60,500]{1,0:T(8,128)} %get-tuple-element.17.mom1, ...), custom_call_target="tpu_custom_call" | custom-call | tf_op jit(solution)/shard_map/codistill/pallas_call | solution.py:313
  110.9 1.7 %copy.12 = f32[1,60,500]{2,0,1:T(1,128)} copy(f32[1,60,500]{2,1,0:T(8,128)} %bitcast.19) | data formatting | bytes 240000
  112.6 1.7 %copy.13 = f32[1,60,500]{2,0,1:T(1,128)} copy(f32[1,60,500]{2,1,0:T(8,128)} %bitcast.18) | data formatting | bytes 240000
  114.3 1.7 %copy.14 = f32[1,60,500]{2,0,1:T(1,128)} copy(f32[1,60,500]{2,1,0:T(8,128)} %bitcast.17) | data formatting | bytes 240000
  116.0 4.3 %copy.23 = bf16[2,1,512,1920]{3,2,1,0:T(8,128)(2,1)} copy(bf16[2,1,512,1920]{3,2,1,0:T(8,128)(2,1)} %bitcast.15) | data formatting | bytes 7864320

commit v2 on v0

v2 whole, which is shorter than its diff:
```python
import jax
import jax.numpy as jnp
from jax import lax
from jax.experimental import pallas as pl
from jax.experimental.pallas import tpu as pltpu
from jax.sharding import Mesh
from jax.sharding import PartitionSpec as P

MESH = pl.DeviceIdType.MESH
F32 = jnp.float32
BF16 = jnp.bfloat16
SEGS = 8
REPS = 8
LANES = 128
UNITS = 4
ROWS = 60
PAD = 64
GROUP = 4 * ROWS
WIDE = 4 * PAD


def packed_of(padded):
    block = sum(jnp.where(padded >= k * PAD, 1, 0) for k in (1, 2, 3))
    inside = padded - block * PAD
    return jnp.where(inside < ROWS, block * ROWS + inside, -1)


def spread(rows, offset):
    at = lax.broadcasted_iota(jnp.int32, (rows, WIDE), 0)
    to = packed_of(lax.broadcasted_iota(jnp.int32, (rows, WIDE), 1))
    return jnp.where((to >= 0) & (at == to + offset), 1.0, 0.0).astype(BF16)


def kernel(
    partners, mask, segs, master, hidden_hbm,
    hg_out, g_out,
    hid, hid_p, hid_t, hp, head, logits, sent, got_0, got_1, got_2, got_3, stage, other, scale, grad,
    dw, r1, s2, r2, s3, r3,
    local_sem, z_s, z_r, a_s, a_r, b_s, b_r, p1_s, p1_r, p2_s, p2_r,
    c_s, c_r, d_s, d_r, e_s, e_r,
):
    zl, co = lax.axis_index("zl"), lax.axis_index("co")
    zh, x, y = lax.axis_index("zh"), lax.axis_index("x"), lax.axis_index("y")
    me = zl * 2 + co
    tokens = hid.shape[0] // 2
    part = tokens // REPS
    got = (got_0, got_1, got_2, got_3)

    load = pltpu.make_async_copy(hidden_hbm, hid, local_sem)
    load.start()

    def rep_of(d):
        to = lax.rem(me + d, REPS)
        return to, {"zl": to // 2, "co": lax.rem(to, 2)}

    def near(axis, d):
        to = lax.rem((x if axis == "x" else y) + d, 4)
        return to, {axis: to}

    across = {"zh": 1 - zh}

    barrier = pltpu.get_barrier_semaphore()
    peers = [across] + [near(a, d)[1] for a in ("x", "y") for d in (1, 2, 3)]
    peers += [rep_of(d)[1] for d in range(1, REPS)]
    for peer in peers:
        pl.semaphore_signal(barrier, inc=1, device_id=peer, device_id_type=MESH)

    low = master[:, 0, :].astype(BF16)
    vocab = low.shape[1]
    for u in range(UNITS):
        cols = min(LANES, vocab - u * LANES)
        piece = low[:, u * LANES : u * LANES + cols]
        if cols < LANES:
            piece = jnp.concatenate([piece, jnp.zeros((ROWS, LANES - cols), BF16)], axis=1)
        piece = jnp.concatenate([piece, jnp.zeros((PAD - ROWS, LANES), BF16)], axis=0)
        hp[u, zh, x, y] = piece

    pl.semaphore_wait(barrier, len(peers))

    started = []

    def send(src, dst, send_sem, recv_sem, peer):
        copy = pltpu.make_async_remote_copy(
            src_ref=src, dst_ref=dst, send_sem=send_sem, recv_sem=recv_sem,
            device_id=peer, device_id_type=MESH,
        )
        copy.start()
        started.append(copy)
        return copy

    def first_leg(u, half, along_x, along_y):
        ref = hp.at[u, half, x, y]
        copies = []
        for d in (1, 2, 3):
            peer = {"x": lax.rem(x + d * along_x, 4), "y": lax.rem(y + d * along_y, 4)}
            copies.append(send(ref, ref, a_s.at[u, half, d - 1], a_r.at[u, half, d - 1], peer))
        return copies

    z_copies, near_copies, far_copies, last_copies = [], [], [], []
    for u in range(UNITS):
        ref = hp.at[u, zh, x, y]
        z_copies.append(send(ref, ref, z_s.at[u], z_r.at[u], across))
        near_copies.append(first_leg(u, zh, 1 - zh, zh))
    for u in range(UNITS):
        z_copies[u].wait_recv()
        far_copies.append(first_leg(u, 1 - zh, zh, 1 - zh))
    for u in range(UNITS):
        for copy in near_copies[u] + far_copies[u]:
            copy.wait_recv()
        group = []
        for half, axis in ((0, "y"), (1, "x")):
            ref = hp.at[u, 0, :, y] if half == 0 else hp.at[u, 1, x]
            for d in (1, 2, 3):
                group.append(
                    send(ref, ref, b_s.at[u, half, d - 1], b_r.at[u, half, d - 1], near(axis, d)[1])
                )
        last_copies.append(group)

    load.wait()
    for g in range(8):
        start = min(g * GROUP // LANES * LANES, hid.shape[1] - 3 * LANES)
        matrix = spread(3 * LANES, g * GROUP - start)

        @pl.loop(0, 4)
        def _(t):
            rows = pl.ds(pl.multiple_of(t * WIDE, WIDE), WIDE)
            block = jnp.dot(hid[rows, start : start + 3 * LANES], matrix, preferred_element_type=F32)
            hid_p[rows, g * WIDE : (g + 1) * WIDE] = block.astype(BF16)

    def forward(u):
        for copy in last_copies[u]:
            copy.wait_recv()

        @pl.loop(0, 4)
        def _(t):
            rows = pl.ds(pl.multiple_of(t * WIDE, WIDE), WIDE)
            weights = hp[u].reshape(8 * WIDE, LANES)
            block = jnp.dot(hid_p[rows, :], weights, preferred_element_type=F32).reshape(4, part, LANES)
            logits[u, pl.ds(lax.rem(t, 2) * 4, 4), t // 2] = block
            sent[u, pl.ds(lax.rem(t, 2) * 4, 4), t // 2] = block.astype(BF16)

        copies = []
        for d in range(1, REPS):
            to, peer = rep_of(d)
            copies.append(send(sent.at[u, to], got[u].at[me], p1_s.at[u, d - 1], p1_r.at[u, d - 1], peer))
        got[u][me] = sent[u, me]
        return copies

    def choose(u, copies):
        for copy in copies:
            copy.wait_recv()
        after = []
        for d in range(1, REPS):
            to, peer = rep_of(d)
            for m in range(2):
                stage[u, d - 1, m] = got[u][partners[m, to], m]
            after.append(
                send(stage.at[u, d - 1], other.at[u, me], p2_s.at[u, d - 1], p2_r.at[u, d - 1], peer)
            )
        for m in range(2):
            other[u, me, m] = got[u][partners[m, me], m]
        return after

    def backward(u, copies):
        lanes = slice(u * LANES, (u + 1) * LANES)
        for copy in copies:
            copy.wait_recv()

        @pl.loop(0, REPS)
        def _(k):
            for m in range(2):
                rows = pl.ds(pl.multiple_of((m * REPS + k) * part, part), part)
                diff = logits[u, k, m] - other[u, k, m].astype(F32)
                grad[rows, lanes] = (diff * scale[rows, :]).astype(BF16)

        @pl.loop(0, 8)
        def _(g):
            rows = pl.ds(pl.multiple_of(g * WIDE, WIDE), WIDE)
            block = jnp.dot(hid_t[rows, :], grad[:, lanes], preferred_element_type=F32)
            dw[u, g // 4, lax.rem(g, 4)] = block.astype(BF16).reshape(4, PAD, LANES)

        result = []
        for half, axis in ((0, "y"), (1, "x")):
            group = []
            for d in (1, 2, 3):
                to, peer = near(axis, d)
                ref = dw.at[u, 0, :, to] if half == 0 else dw.at[u, 1, to]
                group.append(
                    send(ref, r1.at[u, half, d - 1], c_s.at[u, half, d - 1], c_r.at[u, half, d - 1], peer)
                )
            result.append(group)
        return result

    def second(u, copies):
        result = []
        for half, axis in ((0, "x"), (1, "y")):
            for copy in copies[half]:
                copy.wait_recv()
            for k in range(4):
                own = dw[u, 0, k, y] if half == 0 else dw[u, 1, x, k]
                total = own.astype(F32)
                for d in range(3):
                    total = total + r1[u, half, d, k].astype(F32)
                s2[u, half, k] = total.astype(BF16)
            group = []
            for d in (1, 2, 3):
                to, peer = near(axis, d)
                group.append(
                    send(
                        s2.at[u, half, to], r2.at[u, half, d - 1],
                        d_s.at[u, half, d - 1], d_r.at[u, half, d - 1], peer,
                    )
                )
            result.append(group)
        return result

    def third(u, copies):
        for half in range(2):
            for copy in copies[half]:
                copy.wait_recv()
            total = s2[u, half, x if half == 0 else y].astype(F32)
            for d in range(3):
                total = total + r2[u, half, d].astype(F32)
            s3[u, half] = total.astype(BF16)
        return send(s3.at[u, 1 - zh], r3.at[u], e_s.at[u], e_r.at[u], across)

    def finish(u, copy):
        copy.wait_recv()
        cols = min(LANES, vocab - u * LANES)
        total = s3[u, zh].astype(F32) + r3[u].astype(F32)
        g_out[:, 0, u * LANES : u * LANES + cols] = total[:ROWS, :cols]

    def pack_head(u):
        matrix = spread(GROUP, 0)

        @pl.loop(0, 8)
        def _(g):
            rows = pl.ds(pl.multiple_of(g * GROUP, 16), GROUP)
            block = hp[u, g // 4, lax.rem(g, 4)].reshape(WIDE, LANES)
            head[rows, u * LANES : (u + 1) * LANES] = jnp.dot(
                matrix, block, preferred_element_type=F32
            ).astype(BF16)

    p1_0 = forward(0)
    p1_1 = forward(1)
    for m in range(2):
        valid = mask[m : m + 1, :].astype(F32)
        ids = segs[m : m + 1, :]
        onehot = (lax.broadcasted_iota(jnp.int32, (SEGS, tokens), 0) == ids).astype(F32)
        counts = jnp.sum(onehot * valid, axis=1, keepdims=True)
        per_frame = jnp.sum(onehot * counts, axis=0, keepdims=True)
        row = valid / jnp.maximum(per_frame, 1.0)
        scale[m * tokens : (m + 1) * tokens, :] = jnp.broadcast_to(row, (LANES, tokens)).T
    p2_0 = choose(0, p1_0)
    p1_2 = forward(2)

    @pl.loop(0, hid_t.shape[0] // LANES)
    def _(j):
        at = pl.ds(pl.multiple_of(j * LANES, LANES), LANES)
        hid_t[at, :] = hid_p[:, at].T

    p2_1 = choose(1, p1_1)
    p1_3 = forward(3)
    for u in range(UNITS):
        pack_head(u)
    c_0 = backward(0, p2_0)
    p2_2 = choose(2, p1_2)
    d_0 = second(0, c_0)
    c_1 = backward(1, p2_1)
    p2_3 = choose(3, p1_3)
    e_0 = third(0, d_0)
    d_1 = second(1, c_1)
    c_2 = backward(2, p2_2)
    e_1 = third(1, d_1)
    finish(0, e_0)
    d_2 = second(2, c_2)
    finish(1, e_1)
    c_3 = backward(3, p2_3)

    def hidden_gradient(t):
        rows = slice(t * WIDE, (t + 1) * WIDE)
        width = 3 * LANES

        @pl.loop(0, hid.shape[1] // width)
        def _(n):
            at = pl.ds(pl.multiple_of(n * width, LANES), width)
            block = lax.dot_general(
                grad[rows, :], head[at, :], (((1,), (1,)), ((), ())), preferred_element_type=F32
            )
            hg_out[rows, at] = block.astype(BF16)

    hidden_gradient(0)
    e_2 = third(2, d_2)
    hidden_gradient(1)
    d_3 = second(3, c_3)
    hidden_gradient(2)
    finish(2, e_2)
    e_3 = third(3, d_3)
    hidden_gradient(3)
    finish(3, e_3)

    for copy in started:
        copy.wait_send()


def per_device(hidden, partners, frame_mask, segment_ids, master, moment_one, moment_two):
    tokens, depth = hidden.shape[2:]
    frames = 2 * tokens
    part = tokens // REPS
    wide = UNITS * LANES
    padded = 8 * WIDE
    vocab = master.shape[2]
    vmem = pl.BlockSpec(memory_space=pltpu.VMEM)
    dma = pltpu.SemaphoreType.DMA
    exchange = (REPS, 2, part, LANES)
    hg, head_grad = pl.pallas_call(
        kernel,
        out_shape=(pltpu.VMEM((frames, depth), BF16), jax.ShapeDtypeStruct((ROWS, 1, vocab), F32)),
        in_specs=[pl.BlockSpec(memory_space=pltpu.SMEM)] + [vmem] * 3 + [pl.BlockSpec(memory_space=pl.ANY)],
        out_specs=(vmem, vmem),
        scratch_shapes=[
            pltpu.VMEM((frames, depth), BF16),
            pltpu.VMEM((frames, padded), BF16),
            pltpu.VMEM((padded, frames), BF16),
            pltpu.VMEM((UNITS, 2, 4, 4, PAD, LANES), BF16),
            pltpu.VMEM((depth, wide), BF16),
            pltpu.VMEM((UNITS, *exchange), F32),
            pltpu.VMEM((UNITS, *exchange), BF16),
            pltpu.VMEM(exchange, BF16),
            pltpu.VMEM(exchange, BF16),
            pltpu.VMEM(exchange, BF16),
            pltpu.VMEM(exchange, BF16),
            pltpu.VMEM((UNITS, REPS - 1, 2, part, LANES), BF16),
            pltpu.VMEM((UNITS, *exchange), BF16),
            pltpu.VMEM((frames, LANES), F32),
            pltpu.VMEM((frames, wide), BF16),
            pltpu.VMEM((UNITS, 2, 4, 4, PAD, LANES), BF16),
            pltpu.VMEM((UNITS, 2, 3, 4, PAD, LANES), BF16),
            pltpu.VMEM((UNITS, 2, 4, PAD, LANES), BF16),
            pltpu.VMEM((UNITS, 2, 3, PAD, LANES), BF16),
            pltpu.VMEM((UNITS, 2, PAD, LANES), BF16),
            pltpu.VMEM((UNITS, PAD, LANES), BF16),
            dma,
            dma((UNITS,)), dma((UNITS,)),
            dma((UNITS, 2, 3)), dma((UNITS, 2, 3)),
            dma((UNITS, 2, 3)), dma((UNITS, 2, 3)),
            dma((UNITS, 7)), dma((UNITS, 7)),
            dma((UNITS, 7)), dma((UNITS, 7)),
            dma((UNITS, 2, 3)), dma((UNITS, 2, 3)),
            dma((UNITS, 2, 3)), dma((UNITS, 2, 3)),
            dma((UNITS,)), dma((UNITS,)),
        ],
        compiler_params=pltpu.CompilerParams(
            collective_id=0, has_side_effects=True, vmem_limit_bytes=52 << 20
        ),
        name="codistill",
    )(
        partners, frame_mask, segment_ids, master.reshape(ROWS, 1, vocab), hidden.reshape(frames, depth),
    )
    head_grad = head_grad.reshape(master.shape)
    new_moment_one = 0.9 * moment_one + 0.1 * head_grad
    new_moment_two = 0.99 * moment_two + 0.01 * head_grad * head_grad
    new_master = master - 0.01 * new_moment_one / (jnp.sqrt(new_moment_two) + 1e-08)
    return hg.reshape(hidden.shape), new_master, new_moment_one, new_moment_two


def solution(mesh):
    axes = ("zl", "co", "zh", "x", "y")
    torus = Mesh(mesh.devices.reshape(4, 2, 2, 4, 4), axes)
    rep, dp = ("zl", "co"), ("zh", "x", "y")
    in_specs = (
        P(None, rep, dp, None),
        P(),
        P(None, dp),
        P(None, dp),
        P(rep, dp, None),
        P(rep, dp, None),
        P(rep, dp, None),
    )
    out_specs = (
        P(None, rep, dp, None),
        P(rep, dp, None),
        P(rep, dp, None),
        P(rep, dp, None),
    )
    return jax.shard_map(
        per_device, mesh=torus, in_specs=in_specs, out_specs=out_specs, check_vma=False
    )
```

time: 342 us -> 105 us (0.31)
  waiting for transfers between devices: 247 us -> 0 us
  Pallas kernels: 0 us -> 100 us
  local copies, waits for them, and re-layouts: 28.6 us -> 1.95 us
  blocking collectives: 23.9 us -> 0 us
  matrix products: 15.2 us -> 0 us
  between operations: 15.5 us -> 0.68 us
  other arithmetic: 6.99 us -> 1.43 us
    all_gather x2 -> x0, waiting for transfers between devices: 122 us -> none  [the longest x1 88.5 us: per_device(): piece = lax.all_gather(sent, 'rep', axis=0, tiled=True)]
    unnamed x7 -> x0, waiting for transfers between devices: 109 us -> none
    pallas_call x0 -> x1, Pallas kernels: none -> 100 us  [per_device(): pl.pallas_call(kernel, out_shape=(pltpu.VMEM((frames, depth), BF16), jax....]
    all_gather x2 -> x0, blocking collectives: 23.9 us -> none  [gather_in_order(): tiles = lax.all_gather(tiles, axes[k])]
    reduce_scatter x1 -> x0, waiting for transfers between devices: 16 us -> none  [sum_in_order(): tiles = lax.psum_scatter(tiles, axes[k], scatter_dimension=0, tiled=True)]
    dot_general x3 -> x0, matrix products: 15.2 us -> none  [the longest x1 6.14 us: per_device(): logits = jnp.dot(frames_all, head_full, preferred_element_type=jnp.float32)]
    unnamed x28 -> x9, local copies, waits for them, and re-layouts: 7.46 us -> 1.95 us
    dot_general x1 -> x0, other arithmetic: 5.34 us -> none  [per_device(): jnp.einsum('km,kmtv->mtv', selector, piece, preferred_element_type=jnp.fl...]
  transfers between devices with their start and end apart: 5 -> 0, of which waited for: 5 -> 0; matrix products, arithmetic and copies ran while one was open for 2% -> 0% of each run, Pallas kernels for 0% -> 0%
where the time goes in v2:
time: 105 us; the launch traced here: 104 us
  Pallas kernels  100 us (95%)
  local copies, waits for them, and re-layouts  1.95 us (2%)
  other arithmetic  1.43 us (1%)
    pallas_call x1, Pallas kernels, per_device(): pl.pallas_call(kernel, out_shape=(pltpu.VMEM((frames, depth), BF16), jax....  100 us

profile of v2, /device:TPU:32, one launch (start us, length us, event | category | flops | bytes accessed | tf_op | source)
XLA Modules:
  0.0 104.5 jit_solution(6550034804716125138)
XLA Ops:
  0.6 100.4 %codistill.1 = (bf16[1024,1920]{1,0:T(8,128)(2,1)S(1)}, f32[60,1,500]{2,1,0:T(1,128)}) custom-call(s32[2,8]{1,0:T(2,128)} %partners.1, s32[2,512]{1,0:T(2,128)} %mask.1, s32[2,512]{1,0:T(2,128)} %segs.1, f32[60,1,500]{2,1,0:T(1,128)} %bitcast.14, bf16[1024,1920]{1,0:T(8,128)(2,1)} %bitcast.13), custom_call_target="tpu_custom_call" | custom-call | tf_op jit(solution)/shard_map/codistill/pallas_call | solution.py:316
  101.1 0.0 copy-start
  101.1 0.0 copy-start.1
  101.1 0.0 copy-start.2
  101.1 0.0 copy-start.3
  101.1 1.9 %copy.13 = bf16[2,1,512,1920]{3,2,1,0:T(8,128)(2,1)} copy(bf16[2,1,512,1920]{3,2,1,0:T(8,128)(2,1)S(1)} %bitcast.12) | data formatting | bytes 7864320
  103.0 0.0 copy-done
  103.0 0.0 copy-done.1
  103.1 0.0 copy-done.2
  103.1 0.0 copy-done.3
  103.1 1.4 %divide_subtract_fusion = (f32[1,60,500]{2,0,1:T(1,128)}, f32[1,60,500]{2,0,1:T(1,128)}, f32[1,60,500]{2,0,1:T(1,128)}) fusion(f32[1,60,500]{2,0,1:T(1,128)S(1)} %copy-done, f32[60,1,500]{2,1,0:T(1,128)S(1)} %copy-done.3, f32[1,60,500]{2,0,1:T(1,128)S(1)} %copy-done.1, f32[1,60,500]{2,0,1:T(1,128)S(1)} %copy-done.2), kind=kLoop, calls=%fused_computation.4 | loop fusion | flops 330000 | bytes 840000 | tf_op jit(solution)/shard_map/sub | solution.py:363
Async XLA Ops:
  101.1 2.0 %copy-start = (f32[1,60,500]{2,0,1:T(1,128)S(1)}, f32[1,60,500]{2,0,1:T(1,128)}, u32[]{:S(2)}) copy-start(f32[1,60,500]{2,0,1:T(1,128)} %param.11) | copy-start | bytes 360004
  101.1 2.0 %copy-start.1 = (f32[1,60,500]{2,0,1:T(1,128)S(1)}, f32[1,60,500]{2,0,1:T(1,128)}, u32[]{:S(2)}) copy-start(f32[1,60,500]{2,0,1:T(1,128)} %param.12) | copy-start | bytes 360004
  101.1 2.0 %copy-start.2 = (f32[1,60,500]{2,0,1:T(1,128)S(1)}, f32[1,60,500]{2,0,1:T(1,128)}, u32[]{:S(2)}) copy-start(f32[1,60,500]{2,0,1:T(1,128)} %param.13) | copy-start | bytes 360004
  101.1 1.9 %copy-start.3 = (f32[60,1,500]{2,1,0:T(1,128)S(1)}, f32[60,1,500]{2,1,0:T(1,128)}, u32[]{:S(2)}) copy-start(f32[60,1,500]{2,1,0:T(1,128)} %get-tuple-element.7) | copy-start | bytes 360004

commit v3 on v2

v3 whole, which is shorter than its diff:
```python
import jax
import jax.numpy as jnp
from jax import lax
from jax.experimental import pallas as pl
from jax.experimental.pallas import tpu as pltpu
from jax.sharding import Mesh
from jax.sharding import PartitionSpec as P

MESH = pl.DeviceIdType.MESH
F32 = jnp.float32
BF16 = jnp.bfloat16
SEGS = 8
REPS = 8
LANES = 128
UNITS = 4
ROWS = 60
PAD = 64
GROUP = 4 * ROWS
WIDE = 4 * PAD


def spread(rows, offset, stride):
    at = lax.broadcasted_iota(jnp.int32, (rows, WIDE), 0)
    to = lax.broadcasted_iota(jnp.int32, (rows, WIDE), 1)
    block = sum(jnp.where(to >= k * PAD, 1, 0) for k in (1, 2, 3))
    inside = to - block * PAD
    return jnp.where((inside < ROWS) & (at == offset + block * stride + inside), 1.0, 0.0).astype(BF16)


def kernel(
    partners, mask_hbm, segs_hbm, master_hbm, hidden_hbm,
    hg_out, g_out,
    mask, segs, master, hid, hid_p, hid_t, hp, head, logits, sent, got_0, got_1, got_2, got_3, stage, other, scale, grad,
    dw, r1, s2, r2, s3, r3,
    local_sem, z_s, z_r, a_s, a_r, b_s, b_r, p1_s, p1_r, p2_s, p2_r,
    c_s, c_r, d_s, d_r, e_s, e_r,
):
    zl, co = lax.axis_index("zl"), lax.axis_index("co")
    zh, x, y = lax.axis_index("zh"), lax.axis_index("x"), lax.axis_index("y")
    me = zl * 2 + co
    tokens = hid.shape[0] // 2
    part = tokens // REPS
    got = (got_0, got_1, got_2, got_3)

    def rep_of(d):
        to = lax.rem(me + d, REPS)
        return to, {"zl": to // 2, "co": lax.rem(to, 2)}

    def first_of(q):
        return x * (1 - q) + y * q

    def second_of(q):
        return y * (1 - q) + x * q

    def on_first(q, d):
        return lax.rem(first_of(q) + d, 4), {"x": lax.rem(x + d * (1 - q), 4), "y": lax.rem(y + d * q, 4)}

    def on_second(q, d):
        return lax.rem(second_of(q) + d, 4), {"x": lax.rem(x + d * q, 4), "y": lax.rem(y + d * (1 - q), 4)}

    across = {"zh": 1 - zh}

    barrier = pltpu.get_barrier_semaphore()
    peers = [across] + [side(0, d)[1] for side in (on_first, on_second) for d in (1, 2, 3)]
    peers += [rep_of(d)[1] for d in range(1, REPS)]
    for peer in peers:
        pl.semaphore_signal(barrier, inc=1, device_id=peer, device_id_type=MESH)

    loads = []
    for i, (src, dst) in enumerate(((master_hbm, master), (hidden_hbm, hid), (mask_hbm, mask), (segs_hbm, segs))):
        copy = pltpu.make_async_copy(src, dst, local_sem.at[i])
        copy.start()
        loads.append(copy)

    loads[0].wait()
    low = master[:, 0, :].astype(BF16)
    vocab = low.shape[1]
    for u in range(UNITS):
        cols = min(LANES, vocab - u * LANES)
        piece = low[:, u * LANES : u * LANES + cols]
        if cols < LANES:
            piece = jnp.concatenate([piece, jnp.zeros((ROWS, LANES - cols), BF16)], axis=1)
        piece = jnp.concatenate([piece, jnp.zeros((PAD - ROWS, LANES), BF16)], axis=0)
        hp[u, zh, first_of(zh), second_of(zh)] = piece

    pl.semaphore_wait(barrier, len(peers))

    started = []

    def send(src, dst, send_sem, recv_sem, peer):
        copy = pltpu.make_async_remote_copy(
            src_ref=src, dst_ref=dst, send_sem=send_sem, recv_sem=recv_sem,
            device_id=peer, device_id_type=MESH,
        )
        copy.start()
        started.append(copy)
        return copy

    def leg_one(q):
        ref = hp.at[:, q, first_of(q), second_of(q)]
        return [
            send(ref, ref, a_s.at[q, d - 1], a_r.at[q, d - 1], on_first(q, d)[1]) for d in (1, 2, 3)
        ]

    legs = {}

    def leg_two(q, far, k):
        lo, hi = ((0, 1), (1, 2), (2, 4))[k]
        ref = hp.at[lo:hi, q, :, second_of(q)]
        legs[far, k] = [
            send(ref, ref, b_s.at[q, k, d - 1], b_r.at[q, k, d - 1], on_second(q, d)[1]) for d in (1, 2, 3)
        ]

    def arrived(copies):
        for copy in copies:
            copy.wait_recv()

    def pad_hidden(q, k):
        if q == 0:
            width, begin, stride = 3 * LANES, k * GROUP, ROWS
        else:
            width, begin, stride = 8 * LANES, 4 * GROUP + k * ROWS, GROUP
        start = min(begin // LANES * LANES, hid.shape[1] - width)
        matrix = spread(width, begin - start, stride)
        to = (4 * q + k) * WIDE

        @pl.loop(0, 4)
        def _(t):
            rows = pl.ds(pl.multiple_of(t * WIDE, WIDE), WIDE)
            block = jnp.dot(hid[rows, start : start + width], matrix, preferred_element_type=F32)
            hid_p[rows, to : to + WIDE] = block.astype(BF16)

    near_q, far_q = zh, 1 - zh
    near_one = leg_one(near_q)
    own = hp.at[:, zh, first_of(zh), second_of(zh)]
    z_copy = send(own, own, z_s, z_r, across)
    loads[1].wait()
    pad_hidden(0, 0)
    arrived(near_one)
    leg_two(near_q, 0, 0)
    pad_hidden(0, 1)
    arrived([z_copy])
    far_one = leg_one(far_q)
    leg_two(near_q, 0, 1)
    pad_hidden(0, 2)
    pad_hidden(0, 3)
    arrived(far_one)
    leg_two(far_q, 1, 0)
    leg_two(far_q, 1, 1)
    leg_two(near_q, 0, 2)
    leg_two(far_q, 1, 2)
    for k in range(4):
        pad_hidden(1, k)

    def forward(u):
        if u < 3:
            arrived(legs[0, u] + legs[1, u])

        @pl.loop(0, 4)
        def _(t):
            rows = pl.ds(pl.multiple_of(t * WIDE, WIDE), WIDE)
            weights = hp[u].reshape(8 * WIDE, LANES)
            block = jnp.dot(hid_p[rows, :], weights, preferred_element_type=F32).reshape(4, part, LANES)
            logits[u, pl.ds(lax.rem(t, 2) * 4, 4), t // 2] = block
            sent[u, pl.ds(lax.rem(t, 2) * 4, 4), t // 2] = block.astype(BF16)

        copies = []
        for d in range(1, REPS):
            to, peer = rep_of(d)
            copies.append(send(sent.at[u, to], got[u].at[me], p1_s.at[u, d - 1], p1_r.at[u, d - 1], peer))
        got[u][me] = sent[u, me]
        return copies

    def choose(u, copies):
        arrived(copies)
        after = []
        for d in range(1, REPS):
            to, peer = rep_of(d)
            for m in range(2):
                stage[u, d - 1, m] = got[u][partners[m, to], m]
            after.append(
                send(stage.at[u, d - 1], other.at[u, me], p2_s.at[u, d - 1], p2_r.at[u, d - 1], peer)
            )
        for m in range(2):
            other[u, me, m] = got[u][partners[m, me], m]
        return after

    def backward(u, copies):
        lanes = slice(u * LANES, (u + 1) * LANES)
        arrived(copies)

        @pl.loop(0, REPS)
        def _(k):
            for m in range(2):
                rows = pl.ds(pl.multiple_of((m * REPS + k) * part, part), part)
                diff = logits[u, k, m] - other[u, k, m].astype(F32)
                grad[rows, lanes] = (diff * scale[rows, :]).astype(BF16)

        @pl.loop(0, 8)
        def _(g):
            rows = pl.ds(pl.multiple_of(g * WIDE, WIDE), WIDE)
            block = jnp.dot(hid_t[rows, :], grad[:, lanes], preferred_element_type=F32)
            dw[u, g // 4, lax.rem(g, 4)] = block.astype(BF16).reshape(4, PAD, LANES)

    groups = ((0, 2), (2, 3), (3, 4))

    def reduce_one(i):
        lo, hi = groups[i]
        result = []
        for q in range(2):
            copies = []
            for d in (1, 2, 3):
                to, peer = on_second(q, d)
                copies.append(
                    send(
                        dw.at[lo:hi, q, :, to], r1.at[q, d - 1, lo:hi],
                        c_s.at[i, q, d - 1], c_r.at[i, q, d - 1], peer,
                    )
                )
            result.append(copies)
        return result

    def reduce_two(i, before):
        lo, hi = groups[i]
        result = []
        for q in range(2):
            arrived(before[q])
            for u in range(lo, hi):
                for k in range(4):
                    total = dw[u, q, k, second_of(q)].astype(F32)
                    for d in range(3):
                        total = total + r1[q, d, u, k].astype(F32)
                    s2[u, q, k] = total.astype(BF16)
            copies = []
            for d in (1, 2, 3):
                to, peer = on_first(q, d)
                copies.append(
                    send(
                        s2.at[lo:hi, q, to], r2.at[q, d - 1, lo:hi],
                        d_s.at[i, q, d - 1], d_r.at[i, q, d - 1], peer,
                    )
                )
            result.append(copies)
        return result

    def reduce_three(i, before):
        lo, hi = groups[i]
        for q in range(2):
            arrived(before[q])
            for u in range(lo, hi):
                total = s2[u, q, first_of(q)].astype(F32)
                for d in range(3):
                    total = total + r2[q, d, u].astype(F32)
                s3[u, q] = total.astype(BF16)
        return send(s3.at[lo:hi, 1 - zh], r3.at[lo:hi], e_s.at[i], e_r.at[i], across)

    def finish(i, copy):
        lo, hi = groups[i]
        arrived([copy])
        for u in range(lo, hi):
            cols = min(LANES, vocab - u * LANES)
            total = s3[u, zh].astype(F32) + r3[u].astype(F32)
            g_out[:, 0, u * LANES : u * LANES + cols] = total[:ROWS, :cols]

    def pack_head(u):
        matrix = spread(GROUP, 0, ROWS)
        lanes = slice(u * LANES, (u + 1) * LANES)

        @pl.loop(0, 4)
        def _(k):
            for q in range(2):
                block = hp[u, 0, k] if q == 0 else hp[u, 1, :, k]
                block = jnp.dot(matrix, block.reshape(WIDE, LANES), preferred_element_type=F32)
                head[pl.ds(pl.multiple_of((4 * q + k) * GROUP, 16), GROUP), lanes] = block.astype(BF16)

    p1_0 = forward(0)
    p1_1 = forward(1)
    for load in loads[2:]:
        load.wait()
    for m in range(2):
        valid = mask[m : m + 1, :].astype(F32)
        ids = segs[m : m + 1, :]
        onehot = (lax.broadcasted_iota(jnp.int32, (SEGS, tokens), 0) == ids).astype(F32)
        counts = jnp.sum(onehot * valid, axis=1, keepdims=True)
        per_frame = jnp.sum(onehot * counts, axis=0, keepdims=True)
        row = valid / jnp.maximum(per_frame, 1.0)
        scale[m * tokens : (m + 1) * tokens, :] = jnp.broadcast_to(row, (LANES, tokens)).T
    p2_0 = choose(0, p1_0)
    p1_2 = forward(2)

    @pl.loop(0, hid_t.shape[0] // LANES)
    def _(j):
        at = pl.ds(pl.multiple_of(j * LANES, LANES), LANES)
        hid_t[at, :] = hid_p[:, at].T

    p2_1 = choose(1, p1_1)
    p1_3 = forward(3)
    for u in range(UNITS):
        pack_head(u)
    backward(0, p2_0)
    p2_2 = choose(2, p1_2)
    backward(1, p2_1)
    c_0 = reduce_one(0)
    p2_3 = choose(3, p1_3)
    d_0 = reduce_two(0, c_0)
    backward(2, p2_2)
    c_1 = reduce_one(1)
    e_0 = reduce_three(0, d_0)
    backward(3, p2_3)
    c_2 = reduce_one(2)
    d_1 = reduce_two(1, c_1)
    finish(0, e_0)

    def hidden_gradient(t):
        rows = slice(t * WIDE, (t + 1) * WIDE)
        width = 3 * LANES

        @pl.loop(0, hid.shape[1] // width)
        def _(n):
            at = pl.ds(pl.multiple_of(n * width, LANES), width)
            block = lax.dot_general(
                grad[rows, :], head[at, :], (((1,), (1,)), ((), ())), preferred_element_type=F32
            )
            hg_out[rows, at] = block.astype(BF16)

    hidden_gradient(0)
    e_1 = reduce_three(1, d_1)
    hidden_gradient(1)
    d_2 = reduce_two(2, c_2)
    hidden_gradient(2)
    finish(1, e_1)
    e_2 = reduce_three(2, d_2)
    hidden_gradient(3)
    finish(2, e_2)

    for copy in started:
        copy.wait_send()


def per_device(hidden, partners, frame_mask, segment_ids, master, moment_one, moment_two):
    tokens, depth = hidden.shape[2:]
    frames = 2 * tokens
    part = tokens // REPS
    wide = UNITS * LANES
    padded = 8 * WIDE
    vocab = master.shape[2]
    vmem = pl.BlockSpec(memory_space=pltpu.VMEM)
    dma = pltpu.SemaphoreType.DMA
    exchange = (REPS, 2, part, LANES)
    hg, head_grad = pl.pallas_call(
        kernel,
        out_shape=(pltpu.VMEM((frames, depth), BF16), jax.ShapeDtypeStruct((ROWS, 1, vocab), F32)),
        in_specs=[pl.BlockSpec(memory_space=pltpu.SMEM)] + [pl.BlockSpec(memory_space=pl.ANY)] * 4,
        out_specs=(vmem, vmem),
        scratch_shapes=[
            pltpu.VMEM((2, tokens), jnp.int32),
            pltpu.VMEM((2, tokens), jnp.int32),
            pltpu.VMEM((ROWS, 1, vocab), F32),
            pltpu.VMEM((frames, depth), BF16),
            pltpu.VMEM((frames, padded), BF16),
            pltpu.VMEM((padded, frames), BF16),
            pltpu.VMEM((UNITS, 2, 4, 4, PAD, LANES), BF16),
            pltpu.VMEM((depth, wide), BF16),
            pltpu.VMEM((UNITS, *exchange), F32),
            pltpu.VMEM((UNITS, *exchange), BF16),
            pltpu.VMEM(exchange, BF16),
            pltpu.VMEM(exchange, BF16),
            pltpu.VMEM(exchange, BF16),
            pltpu.VMEM(exchange, BF16),
            pltpu.VMEM((UNITS, REPS - 1, 2, part, LANES), BF16),
            pltpu.VMEM((UNITS, *exchange), BF16),
            pltpu.VMEM((frames, LANES), F32),
            pltpu.VMEM((frames, wide), BF16),
            pltpu.VMEM((UNITS, 2, 4, 4, PAD, LANES), BF16),
            pltpu.VMEM((2, 3, UNITS, 4, PAD, LANES), BF16),
            pltpu.VMEM((UNITS, 2, 4, PAD, LANES), BF16),
            pltpu.VMEM((2, 3, UNITS, PAD, LANES), BF16),
            pltpu.VMEM((UNITS, 2, PAD, LANES), BF16),
            pltpu.VMEM((UNITS, PAD, LANES), BF16),
            dma((4,)),
            dma, dma,
            dma((2, 3)), dma((2, 3)),
            dma((2, 3, 3)), dma((2, 3, 3)),
            dma((UNITS, 7)), dma((UNITS, 7)),
            dma((UNITS, 7)), dma((UNITS, 7)),
            dma((3, 2, 3)), dma((3, 2, 3)),
            dma((3, 2, 3)), dma((3, 2, 3)),
            dma((3,)), dma((3,)),
        ],
        compiler_params=pltpu.CompilerParams(
            collective_id=0, has_side_effects=True, vmem_limit_bytes=52 << 20
        ),
        name="codistill",
    )(
        partners, frame_mask, segment_ids, master.reshape(ROWS, 1, vocab), hidden.reshape(frames, depth),
    )
    head_grad = head_grad.reshape(master.shape)
    new_moment_one = 0.9 * moment_one + 0.1 * head_grad
    new_moment_two = 0.99 * moment_two + 0.01 * head_grad * head_grad
    new_master = master - 0.01 * new_moment_one / (jnp.sqrt(new_moment_two) + 1e-08)
    return hg.reshape(hidden.shape), new_master, new_moment_one, new_moment_two


def solution(mesh):
    axes = ("zl", "co", "zh", "x", "y")
    torus = Mesh(mesh.devices.reshape(4, 2, 2, 4, 4), axes)
    rep, dp = ("zl", "co"), ("zh", "x", "y")
    in_specs = (
        P(None, rep, dp, None),
        P(),
        P(None, dp),
        P(None, dp),
        P(rep, dp, None),
        P(rep, dp, None),
        P(rep, dp, None),
    )
    out_specs = (
        P(None, rep, dp, None),
        P(rep, dp, None),
        P(rep, dp, None),
        P(rep, dp, None),
    )
    return jax.shard_map(
        per_device, mesh=torus, in_specs=in_specs, out_specs=out_specs, check_vma=False
    )
```

time: 105 us -> 105 us (level)
  no operation moved by 1% of the time
where the time goes in v3:
time: 105 us
  Pallas kernels  101 us (96%)
  local copies, waits for them, and re-layouts  1.95 us (2%)
  other arithmetic  1.43 us (1%)
    pallas_call x1, Pallas kernels, per_device(): pl.pallas_call(kernel, out_shape=(pltpu.VMEM((frames, depth), BF16), jax....  101 us

profile of v3, /device:TPU:32, one launch (start us, length us, event | category | flops | bytes accessed | tf_op | source)
XLA Modules:
  0.0 105.4 jit_solution(1470978247161248788)
XLA Ops:
  0.6 101.3 %codistill.1 = (bf16[1024,1920]{1,0:T(8,128)(2,1)S(1)}, f32[60,1,500]{2,1,0:T(1,128)}) custom-call(s32[2,8]{1,0:T(2,128)} %partners.1, s32[2,512]{1,0:T(2,128)} %mask_hbm.1, s32[2,512]{1,0:T(2,128)} %segs_hbm.1, f32[60,1,500]{2,1,0:T(1,128)} %bitcast.14, bf16[1024,1920]{1,0:T(8,128)(2,1)} %bitcast.13), custom_call_target="tpu_custom_call" | custom-call | tf_op jit(solution)/shard_map/codistill/pallas_call | solution.py:350
  101.9 0.0 copy-start
  102.0 0.0 copy-start.1
  102.0 0.0 copy-start.2
  102.0 0.0 copy-start.3
  102.0 1.9 %copy.13 = bf16[2,1,512,1920]{3,2,1,0:T(8,128)(2,1)} copy(bf16[2,1,512,1920]{3,2,1,0:T(8,128)(2,1)S(1)} %bitcast.12) | data formatting | bytes 7864320
  103.9 0.0 copy-done
  103.9 0.0 copy-done.1
  103.9 0.0 copy-done.2
  103.9 0.0 copy-done.3
  103.9 1.4 %divide_subtract_fusion = (f32[1,60,500]{2,0,1:T(1,128)}, f32[1,60,500]{2,0,1:T(1,128)}, f32[1,60,500]{2,0,1:T(1,128)}) fusion(f32[1,60,500]{2,0,1:T(1,128)S(1)} %copy-done, f32[60,1,500]{2,1,0:T(1,128)S(1)} %copy-done.3, f32[1,60,500]{2,0,1:T(1,128)S(1)} %copy-done.1, f32[1,60,500]{2,0,1:T(1,128)S(1)} %copy-done.2), kind=kLoop, calls=%fused_computation.4 | loop fusion | flops 330000 | bytes 840000 | tf_op jit(solution)/shard_map/sub | solution.py:400
Async XLA Ops:
  101.9 2.0 %copy-start = (f32[1,60,500]{2,0,1:T(1,128)S(1)}, f32[1,60,500]{2,0,1:T(1,128)}, u32[]{:S(2)}) copy-start(f32[1,60,500]{2,0,1:T(1,128)} %param.11) | copy-start | bytes 360004
  102.0 2.0 %copy-start.1 = (f32[1,60,500]{2,0,1:T(1,128)S(1)}, f32[1,60,500]{2,0,1:T(1,128)}, u32[]{:S(2)}) copy-start(f32[1,60,500]{2,0,1:T(1,128)} %param.12) | copy-start | bytes 360004
  102.0 2.0 %copy-start.2 = (f32[1,60,500]{2,0,1:T(1,128)S(1)}, f32[1,60,500]{2,0,1:T(1,128)}, u32[]{:S(2)}) copy-start(f32[1,60,500]{2,0,1:T(1,128)} %param.13) | copy-start | bytes 360004
  102.0 1.9 %copy-start.3 = (f32[60,1,500]{2,1,0:T(1,128)S(1)}, f32[60,1,500]{2,1,0:T(1,128)}, u32[]{:S(2)}) copy-start(f32[60,1,500]{2,1,0:T(1,128)} %get-tuple-element.7) | copy-start | bytes 360004

commit v4 on v3

--- a/solution.py
+++ b/solution.py
@@ -19,18 +19,18 @@
 WIDE = 4 * PAD
 
 
-def spread(rows, offset, stride):
-    at = lax.broadcasted_iota(jnp.int32, (rows, WIDE), 0)
-    to = lax.broadcasted_iota(jnp.int32, (rows, WIDE), 1)
-    block = sum(jnp.where(to >= k * PAD, 1, 0) for k in (1, 2, 3))
-    inside = to - block * PAD
-    return jnp.where((inside < ROWS) & (at == offset + block * stride + inside), 1.0, 0.0).astype(BF16)
+def spread(transposed):
+    shape = (WIDE, GROUP) if transposed else (GROUP, WIDE)
+    packed = lax.broadcasted_iota(jnp.int32, shape, 1 if transposed else 0)
+    padded = lax.broadcasted_iota(jnp.int32, shape, 0 if transposed else 1)
+    moved = packed + sum(jnp.where(packed >= k * ROWS, PAD - ROWS, 0) for k in (1, 2, 3))
+    return jnp.where(moved == padded, 1.0, 0.0).astype(BF16)
 
 
 def kernel(
     partners, mask_hbm, segs_hbm, master_hbm, hidden_hbm,
     hg_out, g_out,
-    mask, segs, master, hid, hid_p, hid_t, hp, head, logits, sent, got_0, got_1, got_2, got_3, stage, other, scale, grad,
+    mask, segs, master, hid, hid_t, hp, packing, growing, head, logits, sent, got_0, got_1, got_2, got_3, stage, other, scale, grad,
     dw, r1, s2, r2, s3, r3,
     local_sem, z_s, z_r, a_s, a_r, b_s, b_r, p1_s, p1_r, p2_s, p2_r,
     c_s, c_r, d_s, d_r, e_s, e_r,
@@ -83,6 +83,8 @@
         piece = jnp.concatenate([piece, jnp.zeros((PAD - ROWS, LANES), BF16)], axis=0)
         hp[u, zh, first_of(zh), second_of(zh)] = piece
 
+    packing[...] = spread(False)
+    growing[...] = spread(True)
     pl.semaphore_wait(barrier, len(peers))
 
     started = []
@@ -96,18 +98,22 @@
         started.append(copy)
         return copy
 
-    def leg_one(q):
-        ref = hp.at[:, q, first_of(q), second_of(q)]
+    parts = ((0, 1), (1, UNITS))
+
+    def leg_one(q, i):
+        ref = hp.at[parts[i][0] : parts[i][1], q, first_of(q), second_of(q)]
         return [
-            send(ref, ref, a_s.at[q, d - 1], a_r.at[q, d - 1], on_first(q, d)[1]) for d in (1, 2, 3)
+            send(ref, ref, a_s.at[i, q, d - 1], a_r.at[i, q, d - 1], on_first(q, d)[1]) for d in (1, 2, 3)
         ]
 
-    legs = {}
-
-    def leg_two(q, far, k):
+    def leg_z(i):
+        ref = hp.at[parts[i][0] : parts[i][1], zh, first_of(zh), second_of(zh)]
+        return send(ref, ref, z_s.at[i], z_r.at[i], across)
+
+    def leg_two(q, k):
         lo, hi = ((0, 1), (1, 2), (2, 4))[k]
         ref = hp.at[lo:hi, q, :, second_of(q)]
-        legs[far, k] = [
+        return [
             send(ref, ref, b_s.at[q, k, d - 1], b_r.at[q, k, d - 1], on_second(q, d)[1]) for d in (1, 2, 3)
         ]
 
@@ -115,54 +121,43 @@
         for copy in copies:
             copy.wait_recv()
 
-    def pad_hidden(q, k):
-        if q == 0:
-            width, begin, stride = 3 * LANES, k * GROUP, ROWS
-        else:
-            width, begin, stride = 8 * LANES, 4 * GROUP + k * ROWS, GROUP
-        start = min(begin // LANES * LANES, hid.shape[1] - width)
-        matrix = spread(width, begin - start, stride)
-        to = (4 * q + k) * WIDE
-
-        @pl.loop(0, 4)
-        def _(t):
-            rows = pl.ds(pl.multiple_of(t * WIDE, WIDE), WIDE)
-            block = jnp.dot(hid[rows, start : start + width], matrix, preferred_element_type=F32)
-            hid_p[rows, to : to + WIDE] = block.astype(BF16)
-
-    near_q, far_q = zh, 1 - zh
-    near_one = leg_one(near_q)
-    own = hp.at[:, zh, first_of(zh), second_of(zh)]
-    z_copy = send(own, own, z_s, z_r, across)
+    def sent_all(count):
+        for copy in started[:count]:
+            copy.wait_send()
+        del started[:count]
+
+    near, far = zh, 1 - zh
+    near_a = leg_one(near, 0)
+    z_a = leg_z(0)
+    near_b = leg_one(near, 1)
+    z_b = leg_z(1)
+    arrived(near_a)
+    near_0 = leg_two(near, 0)
+    arrived([z_a])
+    far_a = leg_one(far, 0)
+    arrived(near_b)
+    near_1 = leg_two(near, 1)
+    arrived(far_a)
+    far_0 = leg_two(far, 0)
+    arrived([z_b])
+    far_b = leg_one(far, 1)
     loads[1].wait()
-    pad_hidden(0, 0)
-    arrived(near_one)
-    leg_two(near_q, 0, 0)
-    pad_hidden(0, 1)
-    arrived([z_copy])
-    far_one = leg_one(far_q)
-    leg_two(near_q, 0, 1)
-    pad_hidden(0, 2)
-    pad_hidden(0, 3)
-    arrived(far_one)
-    leg_two(far_q, 1, 0)
-    leg_two(far_q, 1, 1)
-    leg_two(near_q, 0, 2)
-    leg_two(far_q, 1, 2)
-    for k in range(4):
-        pad_hidden(1, k)
 
     def forward(u):
-        if u < 3:
-            arrived(legs[0, u] + legs[1, u])
-
-        @pl.loop(0, 4)
-        def _(t):
-            rows = pl.ds(pl.multiple_of(t * WIDE, WIDE), WIDE)
-            weights = hp[u].reshape(8 * WIDE, LANES)
-            block = jnp.dot(hid_p[rows, :], weights, preferred_element_type=F32).reshape(4, part, LANES)
-            logits[u, pl.ds(lax.rem(t, 2) * 4, 4), t // 2] = block
-            sent[u, pl.ds(lax.rem(t, 2) * 4, 4), t // 2] = block.astype(BF16)
+        lanes = slice(u * LANES, (u + 1) * LANES)
+        for k in range(4):
+            for q in range(2):
+                block = hp[u, 0, k] if q == 0 else hp[u, 1, :, k]
+                block = jnp.dot(packing[...], block.reshape(WIDE, LANES), preferred_element_type=F32)
+                head[(4 * q + k) * GROUP : (4 * q + k + 1) * GROUP, lanes] = block.astype(BF16)
+
+        @pl.loop(0, 2)
+        def _(m):
+            rows = pl.ds(pl.multiple_of(m * tokens, tokens), tokens)
+            block = jnp.dot(hid[rows, :], head[:, lanes], preferred_element_type=F32)
+            block = block.reshape(REPS, part, LANES)
+            logits[u, :, m] = block
+            sent[u, :, m] = block.astype(BF16)
 
         copies = []
         for d in range(1, REPS):
@@ -196,11 +191,15 @@
                 diff = logits[u, k, m] - other[u, k, m].astype(F32)
                 grad[rows, lanes] = (diff * scale[rows, :]).astype(BF16)
 
-        @pl.loop(0, 8)
-        def _(g):
-            rows = pl.ds(pl.multiple_of(g * WIDE, WIDE), WIDE)
-            block = jnp.dot(hid_t[rows, :], grad[:, lanes], preferred_element_type=F32)
-            dw[u, g // 4, lax.rem(g, 4)] = block.astype(BF16).reshape(4, PAD, LANES)
+        for k in range(4):
+            for q in range(2):
+                rows = slice((4 * q + k) * GROUP, (4 * q + k + 1) * GROUP)
+                block = jnp.dot(hid_t[rows, :], grad[:, lanes], preferred_element_type=F32).astype(BF16)
+                block = jnp.dot(growing[...], block, preferred_element_type=F32).astype(BF16)
+                if q == 0:
+                    dw[u, 0, k] = block.reshape(4, PAD, LANES)
+                else:
+                    dw[u, 1, :, k] = block.reshape(4, PAD, LANES)
 
     groups = ((0, 2), (2, 3), (3, 4))
 
@@ -262,19 +261,11 @@
             total = s3[u, zh].astype(F32) + r3[u].astype(F32)
             g_out[:, 0, u * LANES : u * LANES + cols] = total[:ROWS, :cols]
 
-    def pack_head(u):
-        matrix = spread(GROUP, 0, ROWS)
-        lanes = slice(u * LANES, (u + 1) * LANES)
-
-        @pl.loop(0, 4)
-        def _(k):
-            for q in range(2):
-                block = hp[u, 0, k] if q == 0 else hp[u, 1, :, k]
-                block = jnp.dot(matrix, block.reshape(WIDE, LANES), preferred_element_type=F32)
-                head[pl.ds(pl.multiple_of((4 * q + k) * GROUP, 16), GROUP), lanes] = block.astype(BF16)
-
+    arrived(near_0 + far_0)
+    arrived(far_b)
+    far_1 = leg_two(far, 1)
+    near_2 = leg_two(near, 2)
     p1_0 = forward(0)
-    p1_1 = forward(1)
     for load in loads[2:]:
         load.wait()
     for m in range(2):
@@ -285,23 +276,27 @@
         per_frame = jnp.sum(onehot * counts, axis=0, keepdims=True)
         row = valid / jnp.maximum(per_frame, 1.0)
         scale[m * tokens : (m + 1) * tokens, :] = jnp.broadcast_to(row, (LANES, tokens)).T
+    arrived(near_1 + far_1)
+    far_2 = leg_two(far, 2)
+    p1_1 = forward(1)
     p2_0 = choose(0, p1_0)
+    arrived(near_2 + far_2)
     p1_2 = forward(2)
 
     @pl.loop(0, hid_t.shape[0] // LANES)
     def _(j):
         at = pl.ds(pl.multiple_of(j * LANES, LANES), LANES)
-        hid_t[at, :] = hid_p[:, at].T
+        hid_t[at, :] = hid[:, at].T
 
     p2_1 = choose(1, p1_1)
     p1_3 = forward(3)
-    for u in range(UNITS):
-        pack_head(u)
+    early = len(started)
     backward(0, p2_0)
     p2_2 = choose(2, p1_2)
     backward(1, p2_1)
     c_0 = reduce_one(0)
     p2_3 = choose(3, p1_3)
+    sent_all(early)
     d_0 = reduce_two(0, c_0)
     backward(2, p2_2)
     c_1 = reduce_one(1)
@@ -333,8 +328,7 @@
     hidden_gradient(3)
     finish(2, e_2)
 
-    for copy in started:
-        copy.wait_send()
+    sent_all(len(started))
 
 
 def per_device(hidden, partners, frame_mask, segment_ids, master, moment_one, moment_two):
@@ -342,7 +336,6 @@
     frames = 2 * tokens
     part = tokens // REPS
     wide = UNITS * LANES
-    padded = 8 * WIDE
     vocab = master.shape[2]
     vmem = pl.BlockSpec(memory_space=pltpu.VMEM)
     dma = pltpu.SemaphoreType.DMA
@@ -357,9 +350,10 @@
             pltpu.VMEM((2, tokens), jnp.int32),
             pltpu.VMEM((ROWS, 1, vocab), F32),
             pltpu.VMEM((frames, depth), BF16),
-            pltpu.VMEM((frames, padded), BF16),
-            pltpu.VMEM((padded, frames), BF16),
+            pltpu.VMEM((depth, frames), BF16),
             pltpu.VMEM((UNITS, 2, 4, 4, PAD, LANES), BF16),
+            pltpu.VMEM((GROUP, WIDE), BF16),
+            pltpu.VMEM((WIDE, GROUP), BF16),
             pltpu.VMEM((depth, wide), BF16),
             pltpu.VMEM((UNITS, *exchange), F32),
             pltpu.VMEM((UNITS, *exchange), BF16),
@@ -378,8 +372,8 @@
             pltpu.VMEM((UNITS, 2, PAD, LANES), BF16),
             pltpu.VMEM((UNITS, PAD, LANES), BF16),
             dma((4,)),
-            dma, dma,
-            dma((2, 3)), dma((2, 3)),
+            dma((2,)), dma((2,)),
+            dma((2, 2, 3)), dma((2, 2, 3)),
             dma((2, 3, 3)), dma((2, 3, 3)),
             dma((UNITS, 7)), dma((UNITS, 7)),
             dma((UNITS, 7)), dma((UNITS, 7)),

time: 105 us -> 103 us (0.981)
  Pallas kernels: 101 us -> 99.3 us
    pallas_call x1, Pallas kernels: 101 us -> 99.3 us  [per_device(): pl.pallas_call(kernel, out_shape=(pltpu.VMEM((frames, depth), BF16), jax....]
where the time goes in v4:
time: 103 us
  Pallas kernels  99.3 us (96%)
  local copies, waits for them, and re-layouts  1.95 us (2%)
  other arithmetic  1.43 us (1%)
    pallas_call x1, Pallas kernels, per_device(): pl.pallas_call(kernel, out_shape=(pltpu.VMEM((frames, depth), BF16), jax....  99.3 us

profile of v4, /device:TPU:32, one launch (start us, length us, event | category | flops | bytes accessed | tf_op | source)
XLA Modules:
  0.0 103.3 jit_solution(14960847971887265230)
XLA Ops:
  0.6 99.3 %codistill.1 = (bf16[1024,1920]{1,0:T(8,128)(2,1)S(1)}, f32[60,1,500]{2,1,0:T(1,128)}) custom-call(s32[2,8]{1,0:T(2,128)} %partners.1, s32[2,512]{1,0:T(2,128)} %mask_hbm.1, s32[2,512]{1,0:T(2,128)} %segs_hbm.1, f32[60,1,500]{2,1,0:T(1,128)} %bitcast.14, bf16[1024,1920]{1,0:T(8,128)(2,1)} %bitcast.13), custom_call_target="tpu_custom_call" | custom-call | tf_op jit(solution)/shard_map/codistill/pallas_call | solution.py:343
  99.9 0.0 copy-start
  99.9 0.0 copy-start.1
  99.9 0.0 copy-start.2
  100.0 0.0 copy-start.3
  100.0 1.9 %copy.13 = bf16[2,1,512,1920]{3,2,1,0:T(8,128)(2,1)} copy(bf16[2,1,512,1920]{3,2,1,0:T(8,128)(2,1)S(1)} %bitcast.12) | data formatting | bytes 7864320
  101.9 0.0 copy-done
  101.9 0.0 copy-done.1
  101.9 0.0 copy-done.2
  101.9 0.0 copy-done.3
  101.9 1.4 %divide_subtract_fusion = (f32[1,60,500]{2,0,1:T(1,128)}, f32[1,60,500]{2,0,1:T(1,128)}, f32[1,60,500]{2,0,1:T(1,128)}) fusion(f32[1,60,500]{2,0,1:T(1,128)S(1)} %copy-done, f32[60,1,500]{2,1,0:T(1,128)S(1)} %copy-done.3, f32[1,60,500]{2,0,1:T(1,128)S(1)} %copy-done.1, f32[1,60,500]{2,0,1:T(1,128)S(1)} %copy-done.2), kind=kLoop, calls=%fused_computation.4 | loop fusion | flops 330000 | bytes 840000 | tf_op jit(solution)/shard_map/sub | solution.py:394
Async XLA Ops:
  99.9 2.0 %copy-start = (f32[1,60,500]{2,0,1:T(1,128)S(1)}, f32[1,60,500]{2,0,1:T(1,128)}, u32[]{:S(2)}) copy-start(f32[1,60,500]{2,0,1:T(1,128)} %param.11) | copy-start | bytes 360004
  99.9 2.0 %copy-start.1 = (f32[1,60,500]{2,0,1:T(1,128)S(1)}, f32[1,60,500]{2,0,1:T(1,128)}, u32[]{:S(2)}) copy-start(f32[1,60,500]{2,0,1:T(1,128)} %param.12) | copy-start | bytes 360004
  99.9 2.0 %copy-start.2 = (f32[1,60,500]{2,0,1:T(1,128)S(1)}, f32[1,60,500]{2,0,1:T(1,128)}, u32[]{:S(2)}) copy-start(f32[1,60,500]{2,0,1:T(1,128)} %param.13) | copy-start | bytes 360004
  100.0 1.9 %copy-start.3 = (f32[60,1,500]{2,1,0:T(1,128)S(1)}, f32[60,1,500]{2,1,0:T(1,128)}, u32[]{:S(2)}) copy-start(f32[60,1,500]{2,1,0:T(1,128)} %get-tuple-element.7) | copy-start | bytes 360004

commit v5 on v4

--- a/solution.py
+++ b/solution.py
@@ -28,9 +28,9 @@
 
 
 def kernel(
-    partners, mask_hbm, segs_hbm, master_hbm, hidden_hbm,
+    partners_hbm, mask_hbm, segs_hbm, master_hbm, hidden_hbm,
     hg_out, g_out,
-    mask, segs, master, hid, hid_t, hp, packing, growing, head, logits, sent, got_0, got_1, got_2, got_3, stage, other, scale, grad,
+    partners, mask, segs, master, hid, hid_t, hp, packing, growing, head, logits, sent, got_0, got_1, got_2, got_3, stage, other, scale, grad,
     dw, r1, s2, r2, s3, r3,
     local_sem, z_s, z_r, a_s, a_r, b_s, b_r, p1_s, p1_r, p2_s, p2_r,
     c_s, c_r, d_s, d_r, e_s, e_r,
@@ -67,7 +67,7 @@
         pl.semaphore_signal(barrier, inc=1, device_id=peer, device_id_type=MESH)
 
     loads = []
-    for i, (src, dst) in enumerate(((master_hbm, master), (hidden_hbm, hid), (mask_hbm, mask), (segs_hbm, segs))):
+    for i, (src, dst) in enumerate(((master_hbm, master), (hidden_hbm, hid), (mask_hbm, mask), (segs_hbm, segs), (partners_hbm, partners))):
         copy = pltpu.make_async_copy(src, dst, local_sem.at[i])
         copy.start()
         loads.append(copy)
@@ -127,21 +127,20 @@
         del started[:count]
 
     near, far = zh, 1 - zh
+    z_a = leg_z(0)
     near_a = leg_one(near, 0)
-    z_a = leg_z(0)
+    z_b = leg_z(1)
     near_b = leg_one(near, 1)
-    z_b = leg_z(1)
     arrived(near_a)
     near_0 = leg_two(near, 0)
+    loads[1].wait()
     arrived([z_a])
     far_a = leg_one(far, 0)
-    arrived(near_b)
-    near_1 = leg_two(near, 1)
+    arrived([z_b])
+    far_b = leg_one(far, 1)
     arrived(far_a)
     far_0 = leg_two(far, 0)
-    arrived([z_b])
-    far_b = leg_one(far, 1)
-    loads[1].wait()
+    arrived(near_b)
 
     def forward(u):
         lanes = slice(u * LANES, (u + 1) * LANES)
@@ -180,8 +179,9 @@
             other[u, me, m] = got[u][partners[m, me], m]
         return after
 
-    def backward(u, copies):
+    def backward(u, copies, then=None):
         lanes = slice(u * LANES, (u + 1) * LANES)
+        result = []
         arrived(copies)
 
         @pl.loop(0, REPS)
@@ -191,8 +191,8 @@
                 diff = logits[u, k, m] - other[u, k, m].astype(F32)
                 grad[rows, lanes] = (diff * scale[rows, :]).astype(BF16)
 
-        for k in range(4):
-            for q in range(2):
+        for q in range(2):
+            for k in range(4):
                 rows = slice((4 * q + k) * GROUP, (4 * q + k + 1) * GROUP)
                 block = jnp.dot(hid_t[rows, :], grad[:, lanes], preferred_element_type=F32).astype(BF16)
                 block = jnp.dot(growing[...], block, preferred_element_type=F32).astype(BF16)
@@ -200,13 +200,16 @@
                     dw[u, 0, k] = block.reshape(4, PAD, LANES)
                 else:
                     dw[u, 1, :, k] = block.reshape(4, PAD, LANES)
+            if then is not None:
+                result.append(then(q))
+        return result
 
     groups = ((0, 2), (2, 3), (3, 4))
 
     def reduce_one(i):
         lo, hi = groups[i]
-        result = []
-        for q in range(2):
+
+        def half(q):
             copies = []
             for d in (1, 2, 3):
                 to, peer = on_second(q, d)
@@ -216,8 +219,9 @@
                         c_s.at[i, q, d - 1], c_r.at[i, q, d - 1], peer,
                     )
                 )
-            result.append(copies)
-        return result
+            return copies
+
+        return half
 
     def reduce_two(i, before):
         lo, hi = groups[i]
@@ -244,14 +248,19 @@
 
     def reduce_three(i, before):
         lo, hi = groups[i]
-        for q in range(2):
-            arrived(before[q])
+        arrived(before[0] + before[1])
+
+        def sum_half(q):
             for u in range(lo, hi):
                 total = s2[u, q, first_of(q)].astype(F32)
                 for d in range(3):
                     total = total + r2[q, d, u].astype(F32)
                 s3[u, q] = total.astype(BF16)
-        return send(s3.at[lo:hi, 1 - zh], r3.at[lo:hi], e_s.at[i], e_r.at[i], across)
+
+        sum_half(1 - zh)
+        copy = send(s3.at[lo:hi, 1 - zh], r3.at[lo:hi], e_s.at[i], e_r.at[i], across)
+        sum_half(zh)
+        return copy
 
     def finish(i, copy):
         lo, hi = groups[i]
@@ -262,10 +271,11 @@
             g_out[:, 0, u * LANES : u * LANES + cols] = total[:ROWS, :cols]
 
     arrived(near_0 + far_0)
+    near_1 = leg_two(near, 1)
+    p1_0 = forward(0)
     arrived(far_b)
     far_1 = leg_two(far, 1)
     near_2 = leg_two(near, 2)
-    p1_0 = forward(0)
     for load in loads[2:]:
         load.wait()
     for m in range(2):
@@ -293,16 +303,13 @@
     early = len(started)
     backward(0, p2_0)
     p2_2 = choose(2, p1_2)
-    backward(1, p2_1)
-    c_0 = reduce_one(0)
+    c_0 = backward(1, p2_1, reduce_one(0))
     p2_3 = choose(3, p1_3)
     sent_all(early)
     d_0 = reduce_two(0, c_0)
-    backward(2, p2_2)
-    c_1 = reduce_one(1)
+    c_1 = backward(2, p2_2, reduce_one(1))
     e_0 = reduce_three(0, d_0)
-    backward(3, p2_3)
-    c_2 = reduce_one(2)
+    c_2 = backward(3, p2_3, reduce_one(2))
     d_1 = reduce_two(1, c_1)
     finish(0, e_0)
 
@@ -343,9 +350,10 @@
     hg, head_grad = pl.pallas_call(
         kernel,
         out_shape=(pltpu.VMEM((frames, depth), BF16), jax.ShapeDtypeStruct((ROWS, 1, vocab), F32)),
-        in_specs=[pl.BlockSpec(memory_space=pltpu.SMEM)] + [pl.BlockSpec(memory_space=pl.ANY)] * 4,
+        in_specs=[pl.BlockSpec(memory_space=pl.ANY)] * 5,
         out_specs=(vmem, vmem),
         scratch_shapes=[
+            pltpu.SMEM((2, REPS), jnp.int32),
             pltpu.VMEM((2, tokens), jnp.int32),
             pltpu.VMEM((2, tokens), jnp.int32),
             pltpu.VMEM((ROWS, 1, vocab), F32),
@@ -371,7 +379,7 @@
             pltpu.VMEM((2, 3, UNITS, PAD, LANES), BF16),
             pltpu.VMEM((UNITS, 2, PAD, LANES), BF16),
             pltpu.VMEM((UNITS, PAD, LANES), BF16),
-            dma((4,)),
+            dma((5,)),
             dma((2,)), dma((2,)),
             dma((2, 2, 3)), dma((2, 2, 3)),
             dma((2, 3, 3)), dma((2, 3, 3)),

time: 103 us -> 101 us (0.981)
  Pallas kernels: 99.3 us -> 97.3 us
    pallas_call x1, Pallas kernels: 99.3 us -> 97.3 us  [per_device(): pl.pallas_call(kernel, out_shape=(pltpu.VMEM((frames, depth), BF16), jax....]
where the time goes in v5:
time: 101 us
  Pallas kernels  97.3 us (96%)
  local copies, waits for them, and re-layouts  1.95 us (2%)
  other arithmetic  1.43 us (1%)
    pallas_call x1, Pallas kernels, per_device(): pl.pallas_call(kernel, out_shape=(pltpu.VMEM((frames, depth), BF16), jax....  97.3 us

profile of v5, /device:TPU:32, one launch (start us, length us, event | category | flops | bytes accessed | tf_op | source)
XLA Modules:
  0.0 101.4 jit_solution(17025545178120519869)
XLA Ops:
  0.6 97.3 %codistill.1 = (bf16[1024,1920]{1,0:T(8,128)(2,1)S(1)}, f32[60,1,500]{2,1,0:T(1,128)}) custom-call(s32[2,8]{1,0:T(2,128)} %partners_hbm.1, s32[2,512]{1,0:T(2,128)} %mask_hbm.1, s32[2,512]{1,0:T(2,128)} %segs_hbm.1, f32[60,1,500]{2,1,0:T(1,128)} %bitcast.14, bf16[1024,1920]{1,0:T(8,128)(2,1)} %bitcast.13), custom_call_target="tpu_custom_call" | custom-call | tf_op jit(solution)/shard_map/codistill/pallas_call | solution.py:350
  98.0 0.0 copy-start
  98.0 0.0 copy-start.1
  98.0 0.0 copy-start.2
  98.0 0.0 copy-start.3
  98.0 1.9 %copy.13 = bf16[2,1,512,1920]{3,2,1,0:T(8,128)(2,1)} copy(bf16[2,1,512,1920]{3,2,1,0:T(8,128)(2,1)S(1)} %bitcast.12) | data formatting | bytes 7864320
  99.9 0.0 copy-done
  99.9 0.0 copy-done.1
  99.9 0.0 copy-done.2
  99.9 0.0 copy-done.3
  99.9 1.4 %divide_subtract_fusion = (f32[1,60,500]{2,0,1:T(1,128)}, f32[1,60,500]{2,0,1:T(1,128)}, f32[1,60,500]{2,0,1:T(1,128)}) fusion(f32[1,60,500]{2,0,1:T(1,128)S(1)} %copy-done, f32[60,1,500]{2,1,0:T(1,128)S(1)} %copy-done.3, f32[1,60,500]{2,0,1:T(1,128)S(1)} %copy-done.1, f32[1,60,500]{2,0,1:T(1,128)S(1)} %copy-done.2), kind=kLoop, calls=%fused_computation.4 | loop fusion | flops 330000 | bytes 840000 | tf_op jit(solution)/shard_map/sub | solution.py:402
Async XLA Ops:
  98.0 2.0 %copy-start = (f32[1,60,500]{2,0,1:T(1,128)S(1)}, f32[1,60,500]{2,0,1:T(1,128)}, u32[]{:S(2)}) copy-start(f32[1,60,500]{2,0,1:T(1,128)} %param.11) | copy-start | bytes 360004
  98.0 2.0 %copy-start.1 = (f32[1,60,500]{2,0,1:T(1,128)S(1)}, f32[1,60,500]{2,0,1:T(1,128)}, u32[]{:S(2)}) copy-start(f32[1,60,500]{2,0,1:T(1,128)} %param.12) | copy-start | bytes 360004
  98.0 2.0 %copy-start.2 = (f32[1,60,500]{2,0,1:T(1,128)S(1)}, f32[1,60,500]{2,0,1:T(1,128)}, u32[]{:S(2)}) copy-start(f32[1,60,500]{2,0,1:T(1,128)} %param.13) | copy-start | bytes 360004
  98.0 1.9 %copy-start.3 = (f32[60,1,500]{2,1,0:T(1,128)S(1)}, f32[60,1,500]{2,1,0:T(1,128)}, u32[]{:S(2)}) copy-start(f32[60,1,500]{2,1,0:T(1,128)} %get-tuple-element.7) | copy-start | bytes 360004

commit v6 on v5

--- a/solution.py
+++ b/solution.py
@@ -129,17 +129,17 @@
     near, far = zh, 1 - zh
     z_a = leg_z(0)
     near_a = leg_one(near, 0)
-    z_b = leg_z(1)
-    near_b = leg_one(near, 1)
     arrived(near_a)
     near_0 = leg_two(near, 0)
     loads[1].wait()
     arrived([z_a])
     far_a = leg_one(far, 0)
+    z_b = leg_z(1)
+    near_b = leg_one(near, 1)
+    arrived(far_a)
+    far_0 = leg_two(far, 0)
     arrived([z_b])
     far_b = leg_one(far, 1)
-    arrived(far_a)
-    far_0 = leg_two(far, 0)
     arrived(near_b)
 
     def forward(u):
@@ -311,7 +311,6 @@
     e_0 = reduce_three(0, d_0)
     c_2 = backward(3, p2_3, reduce_one(2))
     d_1 = reduce_two(1, c_1)
-    finish(0, e_0)
 
     def hidden_gradient(t):
         rows = slice(t * WIDE, (t + 1) * WIDE)
@@ -326,16 +325,48 @@
             hg_out[rows, at] = block.astype(BF16)
 
     hidden_gradient(0)
+    hidden_gradient(1)
+    hidden_gradient(2)
+    d_2 = reduce_two(2, c_2)
     e_1 = reduce_three(1, d_1)
-    hidden_gradient(1)
-    d_2 = reduce_two(2, c_2)
-    hidden_gradient(2)
+    hidden_gradient(3)
+    e_2 = reduce_three(2, d_2)
+    finish(0, e_0)
     finish(1, e_1)
-    e_2 = reduce_three(2, d_2)
-    hidden_gradient(3)
+    sent_all(len(started))
     finish(2, e_2)
 
-    sent_all(len(started))
+
+def adam(hg, head_grad, master, moment_one, moment_two, hg_out, new_master, new_m1, new_m2, held, sems):
+    height = hg.shape[0] // 4
+    for t in range(4):
+        rows = pl.ds(t * height, height)
+        pltpu.make_async_copy(hg.at[rows], hg_out.at[rows], sems.at[7 + t]).start()
+    loads = [
+        pltpu.make_async_copy(ref, held.at[i], sems.at[i])
+        for i, ref in enumerate((head_grad, master, moment_one, moment_two))
+    ]
+    for load in loads:
+        load.start()
+    for load in loads:
+        load.wait()
+    g = held[0]
+    one = 0.9 * held[2] + 0.1 * g
+    two = 0.99 * held[3] + 0.01 * g * g
+    held[5] = one
+    held[6] = two
+    held[4] = held[1] - 0.01 * one / (jnp.sqrt(two) + 1e-08)
+    stores = [
+        pltpu.make_async_copy(held.at[4 + i], ref, sems.at[4 + i])
+        for i, ref in enumerate((new_master, new_m1, new_m2))
+    ]
+    for store in stores:
+        store.start()
+    for store in stores:
+        store.wait()
+    for t in range(4):
+        rows = pl.ds(t * height, height)
+        pltpu.make_async_copy(hg.at[rows], hg_out.at[rows], sems.at[7 + t]).wait()
 
 
 def per_device(hidden, partners, frame_mask, segment_ids, master, moment_one, moment_two):
@@ -345,11 +376,12 @@
     wide = UNITS * LANES
     vocab = master.shape[2]
     vmem = pl.BlockSpec(memory_space=pltpu.VMEM)
+    hbm = pl.BlockSpec(memory_space=pl.ANY)
     dma = pltpu.SemaphoreType.DMA
     exchange = (REPS, 2, part, LANES)
     hg, head_grad = pl.pallas_call(
         kernel,
-        out_shape=(pltpu.VMEM((frames, depth), BF16), jax.ShapeDtypeStruct((ROWS, 1, vocab), F32)),
+        out_shape=(pltpu.VMEM((frames, depth), BF16), pltpu.VMEM((ROWS, 1, vocab), F32)),
         in_specs=[pl.BlockSpec(memory_space=pl.ANY)] * 5,
         out_specs=(vmem, vmem),
         scratch_shapes=[
@@ -396,11 +428,19 @@
     )(
         partners, frame_mask, segment_ids, master.reshape(ROWS, 1, vocab), hidden.reshape(frames, depth),
     )
-    head_grad = head_grad.reshape(master.shape)
-    new_moment_one = 0.9 * moment_one + 0.1 * head_grad
-    new_moment_two = 0.99 * moment_two + 0.01 * head_grad * head_grad
-    new_master = master - 0.01 * new_moment_one / (jnp.sqrt(new_moment_two) + 1e-08)
-    return hg.reshape(hidden.shape), new_master, new_moment_one, new_moment_two
+    flat = (ROWS, 1, vocab)
+    small = jax.ShapeDtypeStruct(flat, F32)
+    hg, new_master, new_m1, new_m2 = pl.pallas_call(
+        adam,
+        out_shape=(jax.ShapeDtypeStruct(hg.shape, BF16), small, small, small),
+        in_specs=[hbm] * 5,
+        out_specs=(hbm,) * 4,
+        scratch_shapes=[pltpu.VMEM((7, *flat), F32), dma((11,))],
+        compiler_params=pltpu.CompilerParams(vmem_limit_bytes=8 << 20),
+        name="adam",
+    )(hg, head_grad, master.reshape(flat), moment_one.reshape(flat), moment_two.reshape(flat))
+    shape = master.shape
+    return hg.reshape(hidden.shape), new_master.reshape(shape), new_m1.reshape(shape), new_m2.reshape(shape)
 
 
 def solution(mesh):

time: 101 us -> 97.4 us (0.964)
  local copies, waits for them, and re-layouts: 1.95 us -> 0.01 us
  other arithmetic: 1.43 us -> 0 us
    unnamed x9 -> x6, local copies, waits for them, and re-layouts: 1.95 us -> 0.01 us
    sub x1 -> x0, other arithmetic: 1.43 us -> none  [per_device(): master - 0.01 * new_moment_one / (jnp.sqrt(new_moment_two) + 1e-08)]
    pallas_call x1 -> x2, Pallas kernels: 97.3 us -> 96.4 us  [the longest x1 94.3 us: per_device(): pl.pallas_call(kernel, out_shape=(pltpu.VMEM((frames, depth), BF16), pltp...]
where the time goes in v6:
time: 97.4 us; the launch traced here: 97.3 us
  Pallas kernels  96.4 us (99%)
    pallas_call x1, Pallas kernels, per_device(): pl.pallas_call(kernel, out_shape=(pltpu.VMEM((frames, depth), BF16), pltp...  94.3 us
    pallas_call x1, Pallas kernels, per_device(): pl.pallas_call(adam, out_shape=(jax.ShapeDtypeStruct(hg.shape, BF16), sma...  2.13 us

profile of v6, /device:TPU:32, one launch (start us, length us, event | category | flops | bytes accessed | tf_op | source)
XLA Modules:
  0.0 97.3 jit_solution(18203371250002850068)
XLA Ops:
  0.6 0.0 copy-start.2
  0.6 0.0 copy-start.1
  0.7 0.0 copy-start
  0.7 94.3 %codistill.1 = (bf16[1024,1920]{1,0:T(8,128)(2,1)S(1)}, f32[60,1,500]{2,1,0:T(1,128)S(1)}) custom-call(s32[2,8]{1,0:T(2,128)} %partners_hbm.1, s32[2,512]{1,0:T(2,128)} %mask_hbm.1, s32[2,512]{1,0:T(2,128)} %segs_hbm.1, f32[60,1,500]{2,1,0:T(1,128)} %bitcast.10, bf16[1024,1920]{1,0:T(8,128)(2,1)} %bitcast.14), custom_call_target="tpu_custom_call" | custom-call | tf_op jit(solution)/shard_map/codistill/pallas_call | solution.py:382
  95.0 0.0 copy-done.2
  95.0 0.0 copy-done.1
  95.0 0.0 copy-done
  95.0 2.1 %adam.1 = (bf16[1024,1920]{1,0:T(8,128)(2,1)}, f32[60,1,500]{2,1,0:T(1,128)}, f32[60,1,500]{2,1,0:T(1,128)}, f32[60,1,500]{2,1,0:T(1,128)}) custom-call(bf16[1024,1920]{1,0:T(8,128)(2,1)S(1)} %get-tuple-element.10.hg, f32[60,1,500]{2,1,0:T(1,128)S(1)} %get-tuple-element.11.head_grad, f32[60,1,500]{2,1,0:T(1,128)S(1)} %bitcast.11, ...), custom_call_target="tpu_custom_call" | custom-call | tf_op jit(solution)/shard_map/adam/pallas_call | solution.py:433
Async XLA Ops:
  0.6 94.3 %copy-start.2 = (f32[1,60,500]{2,0,1:T(1,128)S(1)}, f32[1,60,500]{2,0,1:T(1,128)}, u32[]{:S(2)}) copy-start(f32[1,60,500]{2,0,1:T(1,128)} %param.13) | copy-start | bytes 360004
  0.6 94.3 %copy-start.1 = (f32[1,60,500]{2,0,1:T(1,128)S(1)}, f32[1,60,500]{2,0,1:T(1,128)}, u32[]{:S(2)}) copy-start(f32[1,60,500]{2,0,1:T(1,128)} %param.12) | copy-start | bytes 360004
  0.7 94.3 %copy-start = (f32[1,60,500]{2,0,1:T(1,128)S(1)}, f32[1,60,500]{2,0,1:T(1,128)}, u32[]{:S(2)}) copy-start(f32[1,60,500]{2,0,1:T(1,128)} %param.11) | copy-start | bytes 360004

commit v7 on v6

--- a/solution.py
+++ b/solution.py
@@ -60,14 +60,17 @@
 
     across = {"zh": 1 - zh}
 
+    loads = [pltpu.make_async_copy(master_hbm, master, local_sem.at[0])]
+    loads[0].start()
+
     barrier = pltpu.get_barrier_semaphore()
-    peers = [across] + [side(0, d)[1] for side in (on_first, on_second) for d in (1, 2, 3)]
-    peers += [rep_of(d)[1] for d in range(1, REPS)]
+    peers = [across] + [rep_of(d)[1] for d in range(1, REPS)]
+    peers += [side(0, d)[1] for side in (on_first, on_second) for d in (2, 1, 3)]
     for peer in peers:
         pl.semaphore_signal(barrier, inc=1, device_id=peer, device_id_type=MESH)
 
-    loads = []
-    for i, (src, dst) in enumerate(((master_hbm, master), (hidden_hbm, hid), (mask_hbm, mask), (segs_hbm, segs), (partners_hbm, partners))):
+    others = ((hidden_hbm, hid), (mask_hbm, mask), (segs_hbm, segs), (partners_hbm, partners))
+    for i, (src, dst) in enumerate(others, 1):
         copy = pltpu.make_async_copy(src, dst, local_sem.at[i])
         copy.start()
         loads.append(copy)
@@ -83,8 +86,6 @@
         piece = jnp.concatenate([piece, jnp.zeros((PAD - ROWS, LANES), BF16)], axis=0)
         hp[u, zh, first_of(zh), second_of(zh)] = piece
 
-    packing[...] = spread(False)
-    growing[...] = spread(True)
     pl.semaphore_wait(barrier, len(peers))
 
     started = []
@@ -129,20 +130,23 @@
     near, far = zh, 1 - zh
     z_a = leg_z(0)
     near_a = leg_one(near, 0)
+    z_b = leg_z(1)
+    packing[...] = spread(False)
     arrived(near_a)
     near_0 = leg_two(near, 0)
     loads[1].wait()
     arrived([z_a])
     far_a = leg_one(far, 0)
-    z_b = leg_z(1)
     near_b = leg_one(near, 1)
+    growing[...] = spread(True)
     arrived(far_a)
     far_0 = leg_two(far, 0)
     arrived([z_b])
     far_b = leg_one(far, 1)
     arrived(near_b)
-
-    def forward(u):
+    near_1 = leg_two(near, 1)
+
+    def forward(u, between=None):
         lanes = slice(u * LANES, (u + 1) * LANES)
         for k in range(4):
             for q in range(2):
@@ -158,6 +162,8 @@
             logits[u, :, m] = block
             sent[u, :, m] = block.astype(BF16)
 
+        if between is not None:
+            between()
         copies = []
         for d in range(1, REPS):
             to, peer = rep_of(d)
@@ -271,10 +277,13 @@
             g_out[:, 0, u * LANES : u * LANES + cols] = total[:ROWS, :cols]
 
     arrived(near_0 + far_0)
-    near_1 = leg_two(near, 1)
-    p1_0 = forward(0)
-    arrived(far_b)
-    far_1 = leg_two(far, 1)
+    far_1 = []
+
+    def chunk_one():
+        arrived(far_b)
+        far_1.extend(leg_two(far, 1))
+
+    p1_0 = forward(0, chunk_one)
     near_2 = leg_two(near, 2)
     for load in loads[2:]:
         load.wait()

time: 97.4 us -> 98.7 us (1.013)
  Pallas kernels: 96.4 us -> 97.7 us
    pallas_call x1, Pallas kernels: 94.3 us -> 95.6 us  [per_device(): pl.pallas_call(kernel, out_shape=(pltpu.VMEM((frames, depth), BF16), pltp...]
where the time goes in v7:
time: 98.7 us; the launch traced here: 98.6 us
  Pallas kernels  97.7 us (99%)
    pallas_call x1, Pallas kernels, per_device(): pl.pallas_call(kernel, out_shape=(pltpu.VMEM((frames, depth), BF16), pltp...  95.6 us
    pallas_call x1, Pallas kernels, per_device(): pl.pallas_call(adam, out_shape=(jax.ShapeDtypeStruct(hg.shape, BF16), sma...  2.13 us

profile of v7, /device:TPU:32, one launch (start us, length us, event | category | flops | bytes accessed | tf_op | source)
XLA Modules:
  0.0 98.6 jit_solution(14264130942212267538)
XLA Ops:
  0.6 0.0 copy-start.2
  0.6 0.0 copy-start.1
  0.7 0.0 copy-start
  0.7 95.6 %codistill.1 = (bf16[1024,1920]{1,0:T(8,128)(2,1)S(1)}, f32[60,1,500]{2,1,0:T(1,128)S(1)}) custom-call(s32[2,8]{1,0:T(2,128)} %partners_hbm.1, s32[2,512]{1,0:T(2,128)} %mask_hbm.1, s32[2,512]{1,0:T(2,128)} %segs_hbm.1, f32[60,1,500]{2,1,0:T(1,128)} %bitcast.10, bf16[1024,1920]{1,0:T(8,128)(2,1)} %bitcast.14), custom_call_target="tpu_custom_call" | custom-call | tf_op jit(solution)/shard_map/codistill/pallas_call | solution.py:391
  96.2 0.0 copy-done.2
  96.3 0.0 copy-done.1
  96.3 0.0 copy-done
  96.3 2.1 %adam.1 = (bf16[1024,1920]{1,0:T(8,128)(2,1)}, f32[60,1,500]{2,1,0:T(1,128)}, f32[60,1,500]{2,1,0:T(1,128)}, f32[60,1,500]{2,1,0:T(1,128)}) custom-call(bf16[1024,1920]{1,0:T(8,128)(2,1)S(1)} %get-tuple-element.10.hg, f32[60,1,500]{2,1,0:T(1,128)S(1)} %get-tuple-element.11.head_grad, f32[60,1,500]{2,1,0:T(1,128)S(1)} %bitcast.11, ...), custom_call_target="tpu_custom_call" | custom-call | tf_op jit(solution)/shard_map/adam/pallas_call | solution.py:442
Async XLA Ops:
  0.6 95.6 %copy-start.2 = (f32[1,60,500]{2,0,1:T(1,128)S(1)}, f32[1,60,500]{2,0,1:T(1,128)}, u32[]{:S(2)}) copy-start(f32[1,60,500]{2,0,1:T(1,128)} %param.13) | copy-start | bytes 360004
  0.6 95.6 %copy-start.1 = (f32[1,60,500]{2,0,1:T(1,128)S(1)}, f32[1,60,500]{2,0,1:T(1,128)}, u32[]{:S(2)}) copy-start(f32[1,60,500]{2,0,1:T(1,128)} %param.12) | copy-start | bytes 360004
  0.7 95.6 %copy-start = (f32[1,60,500]{2,0,1:T(1,128)S(1)}, f32[1,60,500]{2,0,1:T(1,128)}, u32[]{:S(2)}) copy-start(f32[1,60,500]{2,0,1:T(1,128)} %param.11) | copy-start | bytes 360004
